TPU v7x, 256 devices: a whole 4x4x8 slice. The times are simulated.
256 devices in a mesh: leaf: 64 (over z, x, core), col: 4 (over y).
Axes of the slice: x: 4, y: 4, z: 8, core: 2. Of those that a mesh axis runs over, the one named last changes fastest.
Arguments:
- leaf_rhs: bfloat16 [64, 2048, 512], P('leaf', 'col'), may hold values from -6 to 6
- leaf_inverse: bfloat16 [64, 2048, 2048], P('leaf', None, 'col'), may hold values from -1 to 2, as said below
- panels: bfloat16 [64, 6, 128, 2048], P('leaf', None, None, 'col'), may hold values from -1 to 1
- pattern: int32 [64, 6], P('leaf'), may hold values 0 or 1
- offsets: int32 [64, 6], P('leaf'), may hold values from 0 to 128
- sep_inverse: float32 [64, 6, 256, 256], P('leaf'), may hold values from -2 to 2, as said below
- sep_link: float32 [64, 5, 256, 256], P('leaf'), may hold values from -1 to 1, as said below
- sep_rhs: float32 [64, 6, 256, 512], P('leaf'), may hold values from -4 to 4, as said below
Outputs:
- leaf_solution: bfloat16 [64, 2048, 512], P('leaf', 'col')
- sep_solution: float32 [64, 6, 256, 512], P('leaf', None, None, 'col')
Inputs may be any that keep to these rules, and one draw needn't show every extreme that they name: `pattern`: 1 where a leaf couples to its ancestor separator of that level, else 0. A coupling block touches rows offsets to offsets + 127 of its separator. `leaf_inverse`: each block is lower triangular with diagonal entries between 0.5 and 1.5. `sep_inverse`: each block is lower triangular with diagonal entries between 0.5 and 1.5; entries [i, k] are equal for all leaves i of one level-k node, the 2^(k+1) leaves that share i // 2^(k+1). `sep_link`: entries [i, k] are equal for all leaves i that share i // 2^(k+1). `sep_rhs`: entries [i, k] are equal for all leaves i that share i // 2^(k+1).
All inputs are finite; a program needn't handle non-finite values. No bound on the sum of `pattern` on one device may be relied on, other than what follows from the above.
Results may differ from a plain program's by a relative error of at most 0.0062.
Values may be sent and summed in bfloat16 or wider, within the bound.
A program may use at most 64 MiB of HBM per device.

v0:
```python
import jax
import jax.numpy as jnp
from jax import lax
from jax.sharding import PartitionSpec as P


def in_blocks(shard, dim, count):
    dims = shard.shape
    tiles = shard.reshape(*dims[:dim], count, dims[dim] // count, *dims[dim + 1 :])
    return jnp.moveaxis(tiles, dim, 0)


def sent_and_summed(shard, axis, dim):
    count = lax.axis_size(axis)
    tiles = lax.all_to_all(in_blocks(shard, dim, count), axis, 0, 0, tiled=True)
    return jnp.sum(tiles, axis=0)


def from_partner(block, axis, stride):
    count = lax.axis_size(axis)
    route = []
    for low in range(count):
        high = low | 1 << stride
        if high != low and high < count:
            route += [(low, high), (high, low)]
    return lax.ppermute(block, axis, route)


def from_everyone(shard, axis):
    copies = jnp.broadcast_to(shard, (lax.axis_size(axis), *shard.shape))
    return lax.all_to_all(copies, axis, split_axis=0, concat_axis=0, tiled=True)


def in_order(tiles, dim):
    tiles = jnp.moveaxis(tiles, 0, dim)
    dims = tiles.shape
    return tiles.reshape(*dims[:dim], dims[dim] * dims[dim + 1], *dims[dim + 2 :])


def gather_directly(shard, axis, dim):
    tiles = from_everyone(shard, axis)
    return in_order(tiles, dim)


def transposed(matrix, vector):
    return lax.dot_general(
        matrix, vector, (((0,), (0,)), ((), ())), precision=lax.Precision.HIGHEST
    )


def on_device(leaf_rhs, leaf_inverse, panels, pattern, offsets, sep_inverse, sep_link, sep_rhs):
    highest = lax.Precision.HIGHEST
    rhs_rows = leaf_rhs[0]
    inverse = leaf_inverse[0]
    leaf_panel = panels[0]
    coupling_on = pattern[0].astype(jnp.float32)
    starts = offsets[0]
    levels = lax.axis_size("leaf").bit_length() - 1
    sources = rhs_rows.shape[1]
    sep_rows = sep_inverse.shape[2]
    touched = leaf_panel.shape[1]
    column = lax.axis_index("col")
    groups = lax.axis_size("col")
    share_cols = sources // groups
    inv_rows = inverse
    solved = sent_and_summed(
        jnp.dot(inv_rows, rhs_rows, preferred_element_type=jnp.float32), "col", 0
    ).astype(jnp.bfloat16)
    partial_value = jnp.einsum(
        "kpr,rn->kpn", leaf_panel, solved, preferred_element_type=jnp.float32
    )
    partial_value = sent_and_summed(partial_value, "col", 2)
    sep_right = lax.dynamic_slice_in_dim(sep_rhs[0], column * share_cols, share_cols, 2)
    placed = []
    for height in range(levels):
        zeros_block = jnp.zeros((sep_rows, share_cols), jnp.float32)
        placed.append(
            lax.dynamic_update_slice(
                zeros_block, coupling_on[height] * partial_value[height], (starts[height], 0)
            )
        )
    update = jnp.stack(placed)
    forward_sols = []
    for height in range(levels):
        remote = from_partner(update[height:], "leaf", height)
        update = update.at[height:].add(remote)
        answer = jnp.dot(
            sep_inverse[0, height], sep_right[height] - update[height], precision=highest
        )
        forward_sols.append(answer)
        if height + 1 < levels:
            update = update.at[height + 1].add(
                jnp.dot(sep_link[0, height], answer, precision=highest)
            )
    backward_sols = [None] * levels
    for height in reversed(range(levels)):
        residue = forward_sols[height]
        if height + 1 < levels:
            residue = residue - transposed(sep_link[0, height], backward_sols[height + 1])
        backward_sols[height] = transposed(sep_inverse[0, height], residue)
    solution = jnp.stack(backward_sols)
    rounded = gather_directly(solution.astype(jnp.bfloat16), "col", 2)
    sliced = jnp.stack(
        [
            lax.dynamic_slice(rounded[height], (starts[height], 0), (touched, sources))
            for height in range(levels)
        ]
    )
    sliced = sliced * pattern[0].astype(jnp.bfloat16)[:, None, None]
    coupled = jnp.einsum("kpr,kpn->rn", leaf_panel, sliced, preferred_element_type=jnp.float32)
    reduced = (solved.astype(jnp.float32) - coupled).astype(jnp.bfloat16)
    inv_rows = inverse
    final = lax.dot_general(
        inv_rows,
        gather_directly(reduced, "col", 0),
        (((0,), (0,)), ((), ())),
        preferred_element_type=jnp.float32,
    )
    return (final.astype(jnp.bfloat16)[None], solution[None])


def solution(mesh):
    in_specs = (
        P("leaf", "col", None),
        P("leaf", None, "col"),
        P("leaf", None, None, "col"),
        P("leaf", None),
        P("leaf", None),
        P("leaf", None, None, None),
        P("leaf", None, None, None),
        P("leaf", None, None, None),
    )
    out_specs = (P("leaf", "col", None), P("leaf", None, None, "col"))
    return jax.shard_map(
        on_device, mesh=mesh, in_specs=in_specs, out_specs=out_specs, check_vma=False
    )
```

profile of v0, /device:TPU:102, one launch (start us, length us, event | category | flops | bytes accessed | tf_op | source)
XLA Modules:
  0.0 263.4 jit_solution(11507331862698009434)
XLA Ops:
  0.6 1.6 copy-done
  2.2 4.3 %fusion.16 = f32[4,512,512]{2,1,0:T(8,128)} fusion(bf16[4,512,512]{2,1,0:T(8,128)(2,1)S(1)} %bitcast.260, bf16[1,512,512]{2,1,0:T(8,128)(2,1)} %param.32), kind=kOutput, calls=%fused_computation.25 | convolution fusion | flops 1073741824 | bytes 6815744 | tf_op jit(solution)/shard_map/dot_general | solution.py:67
  6.5 4.8 %all-to-all-start = ((f32[4,512,512]{2,1,0:T(8,128)}), f32[4,512,512]{2,1,0:T(8,128)}, u32[]{:S(2)}, u32[]{:S(2)}) async-start(f32[4,512,512]{2,1,0:T(8,128)} %fusion.16), calls=%async_computation | async-start | bytes 8388608 | tf_op jit(solution)/shard_map/all_to_all | solution.py:15
  11.4 49.1 %all-to-all-done = f32[4,512,512]{2,1,0:T(8,128)} async-done(((f32[4,512,512]{2,1,0:T(8,128)}), f32[4,512,512]{2,1,0:T(8,128)}, u32[]{:S(2)}, u32[]{:S(2)}) %all-to-all-start) | async-done | bytes 4194336 | tf_op jit(solution)/shard_map/all_to_all | solution.py:15
  60.5 2.7 %reduce_sum.18 = bf16[512,512]{1,0:T(8,128)(2,1)S(1)} reduce(f32[4,512,512]{2,1,0:T(8,128)} %all-to-all-done, f32[]{:T(128)} %constant.298.clone.1), dimensions={0}, to_apply=%region_0.0 | reduce | flops 786432 | bytes 4718596 | tf_op jit(solution)/shard_map/reduce_sum | solution.py:16
  63.5 1.9 fusion.12
  66.7 4.5 %all-to-all-start.1 = ((f32[4,6,128,128]{2,3,1,0:T(8,128)}), f32[4,6,128,128]{2,3,1,0:T(8,128)}, u32[]{:S(2)}, u32[]{:S(2)}) async-start(f32[4,6,128,128]{2,3,1,0:T(8,128)} %bitcast.261), calls=%async_computation.1 | async-start | bytes 3145728 | tf_op jit(solution)/shard_map/all_to_all | solution.py:15
  83.9 7.4 %all-to-all-done.1 = f32[4,6,128,128]{2,3,1,0:T(8,128)} async-done(((f32[4,6,128,128]{2,3,1,0:T(8,128)}), f32[4,6,128,128]{2,3,1,0:T(8,128)}, u32[]{:S(2)}, u32[]{:S(2)}) %all-to-all-start.1) | async-done | bytes 1572896 | tf_op jit(solution)/shard_map/all_to_all | solution.py:15
  91.4 1.5 reduce_sum.19
  92.9 3.8 %slice_multiply_fusion = (f32[1,128,128]{1,2,0:T(8,128)S(1)}, f32[1,128,128]{1,2,0:T(8,128)S(1)}, f32[1,128,128]{1,2,0:T(8,128)S(1)}, f32[1,128,128]{1,2,0:T(8,1...) fusion(f32[6,128,128]{1,2,0:T(8,128)S(1)} %reduce_sum.19, f32[]{:T(128)} %bitcast.18, f32[]{:T(128)} %bitcast.16, ...), kind=kLoop, calls=%fused_computation.122 | loop fusion | flops 98304 | bytes 786456 | tf_op jit(solution)/shard_map/mul | solution.py:79
  102.1 2.1 constant_dynamic-slice_fusion.5
  104.5 1.5 add.113
  107.4 1.4 fusion.90
  110.6 16.2 %collective-permute-done.1 = f32[5,256,128]{1,2,0:T(8,128)} collective-permute-done((f32[5,256,128]{1,2,0:T(8,128)}, f32[5,256,128]{1,2,0:T(8,128)}, u32[]{:S(2)}, u32[]{:S(2)}) %collective-permute-start.1) | collective-permute-done | bytes 655392 | tf_op jit(solution)/shard_map/ppermute | solution.py:26
  131.8 1.4 collective-permute-start.2
  133.3 13.5 %collective-permute-done.2 = f32[4,256,128]{1,2,0:T(8,128)} collective-permute-done((f32[4,256,128]{1,2,0:T(8,128)}, f32[4,256,128]{1,2,0:T(8,128)}, u32[]{:S(2)}, u32[]{:S(2)}) %collective-permute-start.2) | collective-permute-done | bytes 524320 | tf_op jit(solution)/shard_map/ppermute | solution.py:26
  149.4 1.4 fusion.82
  152.3 9.0 %collective-permute-done.3 = f32[3,256,128]{1,2,0:T(8,128)} collective-permute-done((f32[3,256,128]{1,2,0:T(8,128)}, f32[3,256,128]{1,2,0:T(8,128)}, u32[]{:S(2)}, u32[]{:S(2)}) %collective-permute-start.3) | collective-permute-done | bytes 393248 | tf_op jit(solution)/shard_map/ppermute | solution.py:26
  166.0 1.7 copy.25
  167.7 10.9 %collective-permute-done.4 = f32[2,256,128]{1,2,0:T(8,128)S(1)} collective-permute-done((f32[2,256,128]{1,2,0:T(8,128)}, f32[2,256,128]{1,2,0:T(8,128)S(1)}, u32[]{:S(2)}, u32[]{:S(2)}) %collective-permute-start.4) | collective-permute-done | bytes 262176 | tf_op jit(solution)/shard_map/ppermute | solution.py:26
  178.6 1.5 fusion.27
  180.8 2.0 slice_add_fusion
  182.8 4.5 %collective-permute-start.5 = (f32[1,256,128]{1,2,0:T(8,128)}, f32[1,256,128]{1,2,0:T(8,128)}, u32[]{:S(2)}, u32[]{:S(2)}) collective-permute-start(f32[1,256,128]{1,2,0:T(8,128)} %slice_add_fusion), channel_id=1, source_target_pairs={{0,128},{128,0},{4,132},{132,4},{8,136},{136,8},{12,140},{140,12},... | collective-permute-start | bytes 393224 | tf_op jit(solution)/shard_map/ppermute | solution.py:26
  187.3 1.7 copy.26
  189.0 6.1 %collective-permute-done.5 = f32[1,256,128]{1,2,0:T(8,128)} collective-permute-done((f32[1,256,128]{1,2,0:T(8,128)}, f32[1,256,128]{1,2,0:T(8,128)}, u32[]{:S(2)}, u32[]{:S(2)}) %collective-permute-start.5) | collective-permute-done | bytes 131104 | tf_op jit(solution)/shard_map/ppermute | solution.py:26
  195.1 1.5 fusion.21
  202.1 22.6 %all_to_all.20 = bf16[4,6,256,128]{2,3,1,0:T(8,128)(2,1)S(1)} all-to-all(bf16[4,6,256,128]{2,3,1,0:T(8,128)(2,1)S(1)} %broadcast_in_dim.13), channel_id=1, replica_groups=mesh['leaf'=64,'col'=4] {'col'}, dimensions={0} | all-to-all | bytes 3145728 | tf_op jit(solution)/shard_map/all_to_all | solution.py:31
  226.2 1.4 fusion.6
  228.8 1.5 broadcast_in_dim.14
  230.3 4.4 %all-to-all-start.3 = ((bf16[4,512,512]{2,1,0:T(8,128)(2,1)}), bf16[4,512,512]{2,1,0:T(8,128)(2,1)}, u32[]{:S(2)}, u32[]{:S(2)}) async-start(bf16[4,512,512]{2,1,0:T(8,128)(2,1)} %broadcast_in_dim.14), calls=%async_computation.3 | async-start | bytes 4194304 | tf_op jit(solution)/shard_map/all_to_all | solution.py:31
  235.9 23.6 %all-to-all-done.3 = bf16[4,512,512]{2,1,0:T(8,128)(2,1)} async-done(((bf16[4,512,512]{2,1,0:T(8,128)(2,1)}), bf16[4,512,512]{2,1,0:T(8,128)(2,1)}, u32[]{:S(2)}, u32[]{:S(2)}) %all-to-all-start.3) | async-done | bytes 2097184 | tf_op jit(solution)/shard_map/all_to_all | solution.py:31
  259.5 2.9 %fusion.7 = bf16[1,512,512]{1,2,0:T(8,128)(2,1)S(1)} fusion(bf16[2048,512]{1,0:T(8,128)(2,1)} %bitcast.81, bf16[1,2048,512]{2,1,0:T(8,128)(2,1)S(1)} %copy-done), kind=kOutput, calls=%fused_computation.7 | convolution fusion | flops 1074003968 | bytes 4718592 | tf_op jit(solution)/shard_map/dot_general | solution.py:113
  (109 shorter events, 36.0 us)
Async XLA Ops:
  0.6 1.6 copy-start
  6.5 54.0 %all-to-all-start = ((f32[4,512,512]{2,1,0:T(8,128)}), f32[4,512,512]{2,1,0:T(8,128)}, u32[]{:S(2)}, u32[]{:S(2)}) async-start(f32[4,512,512]{2,1,0:T(8,128)} %fusion.16), calls=%async_computation | async-start | bytes 8388608 | tf_op jit(solution)/shard_map/all_to_all | solution.py:15
  63.5 3.2 %copy-start.3 = (bf16[512,512]{0,1:T(8,128)(2,1)}, bf16[512,512]{0,1:T(8,128)(2,1)S(1)}, u32[]{:S(2)}) copy-start(bf16[512,512]{0,1:T(8,128)(2,1)S(1)} %copy.14) | copy-start | bytes 1572868
  66.7 4.5 %copy-start.16 = (s32[1,6]{1,0:T(1,128)S(1)}, s32[1,6]{1,0:T(1,128)}, u32[]{:S(2)}) copy-start(s32[1,6]{1,0:T(1,128)} %param.36) | copy-start | bytes 76
  66.7 16.5 %copy-start.17 = (s32[1,6]{1,0:T(1,128)S(1)}, s32[1,6]{1,0:T(1,128)}, u32[]{:S(2)}) copy-start(s32[1,6]{1,0:T(1,128)} %param.35) | copy-start | bytes 76
  66.7 24.7 %all-to-all-start.1 = ((f32[4,6,128,128]{2,3,1,0:T(8,128)}), f32[4,6,128,128]{2,3,1,0:T(8,128)}, u32[]{:S(2)}, u32[]{:S(2)}) async-start(f32[4,6,128,128]{2,3,1,0:T(8,128)} %bitcast.261), calls=%async_computation.1 | async-start | bytes 3145728 | tf_op jit(solution)/shard_map/all_to_all | solution.py:15
  102.0 2.4 copy-start.12
  102.0 2.5 collective-permute-start
  107.4 3.1 %copy-start.15 = (f32[1,1,256,128]{3,2,1,0:T(8,128)S(1)}, f32[1,1,256,128]{3,2,1,0:T(8,128)}, u32[]{:S(2)}) copy-start(f32[1,1,256,128]{3,2,1,0:T(8,128)} %get-tuple-element.156) | copy-start | bytes 393220
  109.7 17.1 %collective-permute-start.1 = (f32[5,256,128]{1,2,0:T(8,128)}, f32[5,256,128]{1,2,0:T(8,128)}, u32[]{:S(2)}, u32[]{:S(2)}) collective-permute-start(f32[5,256,128]{1,2,0:T(8,128)} %slice.503), channel_id=1, source_target_pairs={{0,8},{8,0},{4,12},{12,4},{16,24},{24,16},{20,28},{28,20},{32,40},... | collective-permute-start | bytes 1966088 | tf_op jit(solution)/shard_map/ppermute | solution.py:26
  129.5 18.5 %copy-start.5 = (f32[128,256]{1,0:T(8,128)}, f32[128,256]{1,0:T(8,128)S(1)}, u32[]{:S(2)}) copy-start(f32[128,256]{1,0:T(8,128)S(1)} %fusion.45) | copy-start | bytes 393220
  131.8 15.0 %collective-permute-start.2 = (f32[4,256,128]{1,2,0:T(8,128)}, f32[4,256,128]{1,2,0:T(8,128)}, u32[]{:S(2)}, u32[]{:S(2)}) collective-permute-start(f32[4,256,128]{1,2,0:T(8,128)} %slice.506), channel_id=1, source_target_pairs={{0,16},{16,0},{4,20},{20,4},{8,24},{24,8},{12,28},{28,12},{32,48},... | collective-permute-start | bytes 1572872 | tf_op jit(solution)/shard_map/ppermute | solution.py:26
  149.4 13.1 %copy-start.7 = (f32[128,256]{1,0:T(8,128)}, f32[128,256]{1,0:T(8,128)S(1)}, u32[]{:S(2)}) copy-start(f32[128,256]{1,0:T(8,128)S(1)} %fusion.39) | copy-start | bytes 393220
  151.5 9.8 %collective-permute-start.3 = (f32[3,256,128]{1,2,0:T(8,128)}, f32[3,256,128]{1,2,0:T(8,128)}, u32[]{:S(2)}, u32[]{:S(2)}) collective-permute-start(f32[3,256,128]{1,2,0:T(8,128)} %slice.509), channel_id=1, source_target_pairs={{0,32},{32,0},{4,36},{36,4},{8,40},{40,8},{12,44},{44,12},{16,48},... | collective-permute-start | bytes 1179656 | tf_op jit(solution)/shard_map/ppermute | solution.py:26
  152.3 10.2 %copy-start.14 = (f32[1,1,256,128]{2,3,1,0:T(8,128)S(1)}, f32[1,1,256,128]{2,3,1,0:T(8,128)}, u32[]{:S(2)}) copy-start(f32[1,1,256,128]{2,3,1,0:T(8,128)} %copy.24) | copy-start | bytes 393220
  163.9 14.7 %copy-start.9 = (f32[128,256]{1,0:T(8,128)}, f32[128,256]{1,0:T(8,128)S(1)}, u32[]{:S(2)}) copy-start(f32[128,256]{1,0:T(8,128)S(1)} %fusion.33) | copy-start | bytes 393220
  166.0 12.5 %collective-permute-start.4 = (f32[2,256,128]{1,2,0:T(8,128)}, f32[2,256,128]{1,2,0:T(8,128)S(1)}, u32[]{:S(2)}, u32[]{:S(2)}) collective-permute-start(f32[2,256,128]{1,2,0:T(8,128)} %slice.512), channel_id=1, source_target_pairs={{0,64},{64,0},{4,68},{68,4},{8,72},{72,8},{12,76},{76,12},{16,80},... | collective-permute-start | bytes 786440 | tf_op jit(solution)/shard_map/ppermute | solution.py:26
  178.6 19.3 %copy-start.2 = (f32[1,5,256,256]{3,2,1,0:T(8,128)S(1)}, f32[1,5,256,256]{3,2,1,0:T(8,128)}, u32[]{:S(2)}) copy-start(f32[1,5,256,256]{3,2,1,0:T(8,128)} %param.38) | copy-start | bytes 3932164
  180.1 0.7 copy-start.11
  182.8 12.3 %collective-permute-start.5 = (f32[1,256,128]{1,2,0:T(8,128)}, f32[1,256,128]{1,2,0:T(8,128)}, u32[]{:S(2)}, u32[]{:S(2)}) collective-permute-start(f32[1,256,128]{1,2,0:T(8,128)} %slice_add_fusion), channel_id=1, source_target_pairs={{0,128},{128,0},{4,132},{132,4},{8,136},{136,8},{12,140},{140,12},... | collective-permute-start | bytes 393224 | tf_op jit(solution)/shard_map/ppermute | solution.py:26
  188.9 10.2 %copy-start.1 = (f32[1,6,256,256]{3,2,1,0:T(8,128)S(1)}, f32[1,6,256,256]{3,2,1,0:T(8,128)}, u32[]{:S(2)}) copy-start(f32[1,6,256,256]{3,2,1,0:T(8,128)} %param.37) | copy-start | bytes 4718596
  188.9 10.5 %copy-start.10 = (f32[128,256]{1,0:T(8,128)S(1)}, f32[128,256]{1,0:T(8,128)}, u32[]{:S(2)}) copy-start(f32[128,256]{1,0:T(8,128)} %copy-done.9) | copy-start | bytes 393220
  196.6 3.4 %copy-start.8 = (f32[128,256]{1,0:T(8,128)S(1)}, f32[128,256]{1,0:T(8,128)}, u32[]{:S(2)}) copy-start(f32[128,256]{1,0:T(8,128)} %copy-done.7) | copy-start | bytes 393220
  199.1 1.5 copy-start.6
  224.9 1.0 copy-start.4
  224.9 1.3 copy-start.13
  230.3 29.2 %all-to-all-start.3 = ((bf16[4,512,512]{2,1,0:T(8,128)(2,1)}), bf16[4,512,512]{2,1,0:T(8,128)(2,1)}, u32[]{:S(2)}, u32[]{:S(2)}) async-start(bf16[4,512,512]{2,1,0:T(8,128)(2,1)} %broadcast_in_dim.14), calls=%async_computation.3 | async-start | bytes 4194304 | tf_op jit(solution)/shard_map/all_to_all | solution.py:31
where the time goes:
time: 265 us; the launch traced here: 263 us
  waiting for transfers between devices  136 us (51%)
  matrix products  31.6 us (12%)
  local copies, waits for them, and re-layouts  26.5 us (10%)
  blocking collectives  22.6 us (9%)
  starting transfers between devices  20.6 us (8%)
  other arithmetic  13.3 us (5%)
  between operations  12.7 us (5%)
    all_to_all x2, waiting for transfers between devices, sent_and_summed(): tiles = lax.all_to_all(in_blocks(shard, dim, count), axis, 0, 0, tiled=True)  56.6 us
    ppermute x6, waiting for transfers between devices, from_partner(): return lax.ppermute(block, axis, route)  55.9 us
    all_to_all x1, waiting for transfers between devices, from_everyone(): return lax.all_to_all(copies, axis, split_axis=0, concat_axis=0, tiled=True)  23.6 us
    all_to_all x1, blocking collectives, from_everyone(): return lax.all_to_all(copies, axis, split_axis=0, concat_axis=0, tiled=True)  22.6 us
    unnamed x58, local copies, waits for them, and re-layouts  10 us
    all_to_all x2, starting transfers between devices, sent_and_summed(): tiles = lax.all_to_all(in_blocks(shard, dim, count), axis, 0, 0, tiled=True)  9.31 us
    dot_general x6, matrix products, on_device(): jnp.dot(sep_inverse[0, height], sep_right[height] - update[height], preci...  8.46 us
    dot_general x5, matrix products, on_device(): jnp.dot(sep_link[0, height], answer, precision=highest)  7.62 us
  transfers between devices with their start and end apart: 9, of which 9 were waited for; matrix products, arithmetic and copies ran while one was open for 3% of the time, Pallas kernels for 0%

commit v1 on v0

v1 whole, which is shorter than its diff:
```python
import functools

import jax
import jax.numpy as jnp
from jax import lax
from jax.experimental import pallas as pl
from jax.experimental.pallas import tpu as pltpu
from jax.sharding import PartitionSpec as P

MESH = pl.DeviceIdType.MESH
F32 = jnp.float32
BF16 = jnp.bfloat16
HOP = BF16
LEVELS = 6
MASKS = (1, 2, 6, 8, 16, 56)
PAIRS = tuple((k, j) for k in range(1, LEVELS) for j in range(k, LEVELS))


def dot_nn(a, b):
    return lax.dot_general(a, b, (((1,), (0,)), ((), ())), preferred_element_type=F32)


def dot_nt(a, b):
    return lax.dot_general(a, b, (((1,), (1,)), ((), ())), preferred_element_type=F32)


def halves(value):
    high = value.astype(BF16)
    return high, (value - high.astype(F32)).astype(BF16)


def wide(value):
    high, low = halves(value)
    return jnp.concatenate([high, low, high], axis=1)


def kernel(
    rhs, inv, pan, pat, off, sinv, slink, srhs, x_out, sol_out,
    rhs_v, inv_v, pan_v, sinv_v, slink_v, srhs_v,
    bt, fp, fsnd, frx, sol_v, cc, cb, prl, psum, prx, pon, meta, metarx, est,
    wf, wi, wg, rt, u, fs, bs, tsnd, trx, ball, soth, sall, redv, xacc,
    ld, f_ss, f_rs, p_ss, p_rs, prx_rs, m_ss, m_rs, t_ss, t_rs, b_ss, b_rs, s_ss, s_rs, r_ss, r_rs,
):
    leaf = lax.axis_index("leaf")
    c = lax.axis_index("col")
    q = lax.rem(leaf, 2)
    base = leaf - q
    c1, c2, c3 = lax.rem(c + 1, 4), lax.rem(c + 2, 4), lax.rem(c + 3, 4)
    rows = 512

    def remote(src, dst, ss, rs, to_leaf, to_col):
        return pltpu.make_async_remote_copy(
            src_ref=src, dst_ref=dst, send_sem=ss, recv_sem=rs,
            device_id=(to_leaf, to_col), device_id_type=MESH,
        )

    sent = []

    def on(cond, fn):
        pl.when(cond)(fn)

    def order(step):
        return jnp.where(c == 0, (2, 1, 3, 0)[step], 3 - step)

    load_rhs = pltpu.make_async_copy(rhs, rhs_v, ld.at[0])
    load_rhs.start()
    load_inv = []
    for step in range(4):
        r = jnp.maximum(order(step), 0)
        load_inv.append(
            pltpu.make_async_copy(inv.at[pl.ds(pl.multiple_of(r * rows, rows), rows)], inv_v.at[r], ld.at[1 + step])
        )
        on(step <= 3 - c, load_inv[step].start)
    load_pan = pltpu.make_async_copy(pan, pan_v, ld.at[5])
    load_pan.start()
    load_sinv = pltpu.make_async_copy(sinv, sinv_v, ld.at[6])
    load_sinv.start()
    load_slink = pltpu.make_async_copy(slink, slink_v, ld.at[7])
    load_slink.start()
    load_srhs = pltpu.make_async_copy(
        srhs.at[:, :, pl.ds(pl.multiple_of(c * 128, 128), 128)], srhs_v, ld.at[8]
    )
    load_srhs.start()

    peers = [(leaf, c1), (leaf, c2), (leaf, c3)]
    peers += [(base + 1 - q, cc_) for cc_ in (c, c1, c2, c3)]
    peers += [(leaf ^ MASKS[k], c) for k in range(1, LEVELS)]
    barrier = pltpu.get_barrier_semaphore()
    for peer in peers:
        pl.semaphore_signal(barrier, inc=1, device_id=peer, device_id_type=MESH)

    for k in range(LEVELS):
        meta[pl.ds(k, 1), :] = jnp.full((1, 256), off[0, k].astype(F32), F32)
        meta[pl.ds(8 + k, 1), :] = jnp.full((1, 256), pat[0, k].astype(F32), F32)

    load_rhs.wait()
    bt[...] = rhs_v[...].T
    pl.semaphore_wait(barrier, len(peers))

    other = base + 1 - q
    send_meta = remote(meta, metarx, m_ss, m_rs, other, c)
    send_meta.start()

    def fmsg(sender, number, src, slot, to_col):
        return (c == sender, remote(src, frx.at[slot], f_ss.at[number], f_rs.at[slot], leaf, to_col))

    msgs = {
        "20A": fmsg(0, 0, fsnd.at[0, 0], 0, 1),
        "20B": fmsg(0, 1, fsnd.at[0, 1], 0, 3),
        "10A": fmsg(0, 2, fsnd.at[1, 0], 1, 1),
        "10B": fmsg(0, 3, fsnd.at[1, 1], 2, 1),
        "30A": fmsg(0, 4, fsnd.at[2, 0], 1, 3),
        "30B": fmsg(0, 5, fsnd.at[2, 1], 2, 3),
        "31A": fmsg(1, 0, fsnd.at[0, 0], 0, 0),
        "31B": fmsg(1, 1, fsnd.at[0, 1], 1, 0),
        "21B": fmsg(1, 2, fsnd.at[1, 1], 0, 2),
        "21A": fmsg(1, 3, fsnd.at[1, 0], 1, 2),
        "32A": fmsg(2, 0, fsnd.at[0, 0], 3, 3),
        "32B": fmsg(2, 1, fsnd.at[0, 1], 4, 3),
        "relay": fmsg(3, 0, frx.at[0], 2, 2),
    }
    now = {
        (0, 0): ("20A", "31A", "32A"),
        (0, 1): ("20B", "31B", "32B"),
        (1, 0): ("10A",),
        (1, 1): ("10B", "21B"),
    }
    for step in range(4):

        def block(step=step):
            load_inv[step].wait()
            r = order(step)
            for h in range(2):
                value = dot_nt(bt[pl.ds(h * 256, 256), :], inv_v[r])
                fp[step, h] = value
                if step < 3:
                    fsnd[step, h] = value.astype(BF16)
                for name in now.get((step, h), ()):
                    cond, copy = msgs[name]
                    on(cond, copy.start)

        on(step <= 3 - c, block)

    load_sinv.wait()
    load_slink.wait()
    load_srhs.wait()
    highest = lax.Precision.HIGHEST

    def table(k, carry):
        ik = sinv_v[k]
        kk = jnp.minimum(k, LEVELS - 2)
        gk = lax.dot_general(
            slink_v[kk], ik, (((1,), (0,)), ((), ())), precision=highest, preferred_element_type=F32
        )
        ih, il = halves(ik)
        gh, gl = halves(gk)
        for at, (hi, lo) in ((0, (ih, il)), (256, (gh, gl))):
            wf[k, pl.ds(at, 256), pl.ds(0, 256)] = hi
            wf[k, pl.ds(at, 256), pl.ds(256, 256)] = hi
            wf[k, pl.ds(at, 256), pl.ds(512, 256)] = lo
        for ref, (hi, lo) in ((wi, (ih, il)), (wg, (gh, gl))):
            ref[k, pl.ds(0, 256), :] = hi
            ref[k, pl.ds(256, 256), :] = hi
            ref[k, pl.ds(512, 256), :] = lo
        rt[k] = srhs_v[k].T
        return carry

    lax.fori_loop(0, LEVELS, table, 0)

    send_meta.wait_recv()
    gap = (
        lax.broadcasted_iota(jnp.int32, (128, 256), 1) - lax.broadcasted_iota(jnp.int32, (128, 256), 0)
    ).astype(F32)
    for k in range(LEVELS):
        for part, ref in enumerate((meta, metarx)):
            spot = jnp.broadcast_to(ref[pl.ds(k, 1), :], (128, 256))
            keep = jnp.broadcast_to(ref[pl.ds(8 + k, 1), :], (128, 256))
            hot = jnp.where(gap == spot, keep, 0.0).astype(BF16)
            est[k, pl.ds(part * 256, 128), :] = hot
            est[k, pl.ds(part * 256 + 128, 128), :] = hot

    def frecv(slot, from_col):
        remote(frx.at[slot], frx.at[slot], f_ss.at[0], f_rs.at[slot], leaf, from_col).wait_recv()

    def after0():
        for h, name in enumerate(("30A", "30B")):
            frecv(h, 1)
            fsnd[2, h] = (fp[2, h] + frx[h].astype(F32)).astype(BF16)
            msgs[name][1].start()
        for h in range(2):
            sol_v[0, h] = fp[3, h].astype(BF16)

    def after1():
        frecv(0, 0)
        fsnd[1, 0] = (fp[1, 0] + frx[0].astype(F32)).astype(BF16)
        msgs["21A"][1].start()
        for h in range(2):
            frecv(1 + h, 0)
            sol_v[1, h] = (fp[2, h] + frx[1 + h].astype(F32)).astype(BF16)

    def after2():
        frecv(1, 1)
        sol_v[2, 0] = (fp[1, 0] + frx[1].astype(F32)).astype(BF16)
        frecv(0, 1)
        frecv(2, 3)
        sol_v[2, 1] = (fp[1, 1] + frx[0].astype(F32) + frx[2].astype(F32)).astype(BF16)

    def after3():
        frecv(0, 0)
        msgs["relay"][1].start()
        for h in range(2):
            frecv(3 + h, 2)
            frecv(1 + h, 0)
            sol_v[3, h] = (fp[0, h] + frx[1 + h].astype(F32) + frx[3 + h].astype(F32)).astype(BF16)

    for group, fn in enumerate((after0, after1, after2, after3)):
        on(c == group, fn)

    load_pan.wait()
    panels = pan_v
    for h in range(2):
        share = dot_nt(sol_v[c, h], panels[...]).reshape(2, 2, 64, 768)
        cc[pl.ds(2 * h, 2)] = share
        cb[pl.ds(2 * h, 2)] = share.astype(BF16)
    relay_up = remote(cb.at[c2, 0], prl.at[0], p_ss.at[0], p_rs.at[0], leaf, c1)
    relay_down = remote(cb.at[c2, 1], prl.at[1], p_ss.at[1], p_rs.at[1], leaf, c3)
    direct_up = remote(cb.at[c1, 1], prx.at[q, 0], p_ss.at[2], prx_rs.at[q, 0], base + 1, c1)
    direct_down = remote(cb.at[c3, 0], prx.at[q, 1], p_ss.at[3], prx_rs.at[q, 1], base, c3)
    across = remote(cb.at[c, 1 - q], pon, p_ss.at[4], p_rs.at[2], other, c)
    sum_up = remote(psum.at[0], prx.at[q, 0], p_ss.at[5], prx_rs.at[q, 0], base, c1)
    sum_down = remote(psum.at[1], prx.at[q, 1], p_ss.at[6], prx_rs.at[q, 1], base + 1, c3)
    for copy in (relay_up, relay_down, direct_up, direct_down, across):
        copy.start()
    relay_up.wait_recv()
    psum[0] = (cc[c1, 0] + prl[0].astype(F32)).astype(BF16)
    sum_up.start()
    relay_down.wait_recv()
    psum[1] = (cc[c3, 1] + prl[1].astype(F32)).astype(BF16)
    sum_down.start()
    across.wait_recv()

    def precv(p, d, from_col):
        remote(prx.at[p, d], prx.at[p, d], p_ss.at[0], prx_rs.at[p, d], base + p, from_col).wait_recv()

    for p in range(2):
        precv(p, 0, c3)
        precv(p, 1, c1)
    mine = cc[c, q] + prx[q, 0].astype(F32) + prx[q, 1].astype(F32)
    theirs = pon[...].astype(F32) + prx[1 - q, 0].astype(F32) + prx[1 - q, 1].astype(F32)
    mh, ml = halves(mine)
    th, tl = halves(theirs)
    for k in range(LEVELS):
        at = slice(k * 128, k * 128 + 128)
        left = jnp.concatenate([mh[:, at], ml[:, at], th[:, at], tl[:, at]], axis=1)
        u[k] = dot_nn(left, est[k])

    mine_rows = pl.ds(pl.multiple_of(q * 64, 64), 64)

    def tree(k, j):
        n = PAIRS.index((k, j))
        return remote(tsnd.at[n], trx.at[n], t_ss.at[n], t_rs.at[n], leaf ^ MASKS[k], c)

    def send(k, j):
        tsnd[PAIRS.index((k, j))] = u[j].astype(HOP)
        tree(k, j).start()

    def receive(k, j):
        tree(k, j).wait_recv()
        u[j] = u[j] + trx[PAIRS.index((k, j))].astype(F32)

    for k in range(LEVELS):
        if k > 0:
            receive(k, k)
        both = dot_nt(wide(rt[k, mine_rows, :] - u[k]), wf[k])
        if k + 1 < LEVELS:
            if k > 0:
                receive(k, k + 1)
            u[k + 1] = u[k + 1] + both[:, 256:]
            send(k + 1, k + 1)
            for j in range(k + 2, LEVELS):
                if k > 0:
                    receive(k, j)
                send(k + 1, j)
        fs[k] = dot_nn(wide(both[:, :256]), wi[k])
    for k in reversed(range(LEVELS)):
        down = fs[k]
        if k + 1 < LEVELS:
            down = down - dot_nn(wide(bs[k + 1]), wg[k])
        bs[k] = down
        ball[k, mine_rows, :] = down

    swap = remote(ball.at[:, mine_rows, :], ball.at[:, mine_rows, :], b_ss, b_rs, other, c)
    slot = c * 2 + q
    for k in range(LEVELS):
        low = bs[k].astype(BF16)
        at = slice(k * 128, k * 128 + 128)
        sall[slot, :, at] = dot_nt(low, est[k, pl.ds(0, 128), :]).astype(BF16)
        soth[:, at] = dot_nt(low, est[k, pl.ds(256, 128), :]).astype(BF16)
    s_copies = [
        remote(sall.at[slot], sall.at[slot], s_ss.at[0], s_rs.at[slot], leaf, c1),
        remote(soth, sall.at[slot], s_ss.at[1], s_rs.at[slot], other, c1),
        remote(sall.at[slot], sall.at[slot], s_ss.at[2], s_rs.at[slot], leaf, c3),
        remote(soth, sall.at[slot], s_ss.at[3], s_rs.at[slot], other, c3),
        remote(soth, sall.at[slot], s_ss.at[4], s_rs.at[slot], other, c),
    ]
    for copy in s_copies:
        copy.start()
    swap.start()

    def srecv(at, from_leaf, from_col):
        remote(sall.at[at], sall.at[at], s_ss.at[0], s_rs.at[at], from_leaf, from_col).wait_recv()

    near, far = jnp.where(q == 0, c3, c1), jnp.where(q == 0, c1, c3)
    relays = []
    for p in range(2):
        at = near * 2 + p
        srecv(at, base + p, near)
        relays.append(remote(sall.at[at], sall.at[at], s_ss.at[5 + p], s_rs.at[at], leaf, far))
        relays[p].start()

    remote(ball.at[:, mine_rows, :], ball.at[:, mine_rows, :], b_ss, b_rs, other, c).wait_send()
    theirs_rows = pl.ds(pl.multiple_of((1 - q) * 64, 64), 64)
    remote(ball.at[:, theirs_rows, :], ball.at[:, theirs_rows, :], b_ss, b_rs, other, c).wait_recv()
    for k in range(LEVELS):
        sol_out[k] = ball[k].T

    srecv(c * 2 + 1 - q, other, c)
    for p in range(2):
        srecv(far * 2 + p, base + p, far)
    for p in range(2):
        srecv(c2 * 2 + p, leaf, near)

    for h in range(2):
        taken = sall[pl.ds(4 * h, 4)].reshape(256, 768)
        redv[c, h] = (sol_v[c, h].astype(F32) - dot_nn(taken, panels[...])).astype(BF16)

    def rmsg(sender, number, r, h, to_col):
        return (c == sender, remote(redv.at[r, h], redv.at[r, h], r_ss.at[number], r_rs.at[r, h], leaf, to_col))

    rfirst = [
        rmsg(3, 0, 3, 1, 0), rmsg(3, 1, 3, 0, 0), rmsg(3, 2, 3, 0, 2), rmsg(3, 3, 3, 1, 2),
        rmsg(2, 0, 2, 1, 3), rmsg(2, 1, 2, 0, 1), rmsg(2, 2, 2, 1, 1),
        rmsg(1, 0, 1, 0, 0), rmsg(1, 1, 1, 1, 0),
    ]
    rnext = [rmsg(3, 4, 2, 1, 0), rmsg(2, 3, 3, 0, 1), rmsg(1, 2, 2, 0, 0), rmsg(0, 0, 3, 1, 1)]
    for cond, copy in rfirst:
        on(cond, copy.start)
    for h in range(2):
        xacc[h] = dot_nn(redv[c, h], inv_v[c])

    def rrecv(r, h):
        remote(redv.at[r, h], redv.at[r, h], r_ss.at[0], r_rs.at[r, h], leaf, c1).wait_recv()

    for (cond, copy), (r, h) in zip(rnext, ((2, 1), (3, 0), (2, 0), (3, 1))):

        def pass_on(copy=copy, r=r, h=h):
            rrecv(r, h)
            copy.start()

        on(cond, pass_on)
    for step in range(1, 4):

        def add(step=step):
            r = c + step
            for h in range(2):
                taken = ((c == 2) & (r == 3) & (h == 0)) | ((c == 1) & (r == 2) & (h == 0)) | ((c == 0) & (r == 3) & (h == 1))
                on(jnp.logical_not(taken), functools.partial(rrecv, r, h))
                xacc[h] += dot_nn(redv[r, h], inv_v[r])

        on(c + step <= 3, add)
    for h in range(2):
        x_out[:, pl.ds(h * 256, 256)] = xacc[h].T.astype(BF16)

    for copy in (send_meta, relay_up, relay_down, direct_up, direct_down, across, sum_up, sum_down, *s_copies, *relays):
        copy.wait_send()
    for k, j in PAIRS:
        tree(k, j).wait_send()
    for cond, copy in (*msgs.values(), *rfirst, *rnext):
        on(cond, copy.wait_send)


def on_device(leaf_rhs, leaf_inverse, panels, pattern, offsets, sep_inverse, sep_link, sep_rhs):
    anywhere = pl.BlockSpec(memory_space=pl.ANY)
    scalars = pl.BlockSpec(memory_space=pltpu.SMEM)
    vmem = pl.BlockSpec(memory_space=pltpu.VMEM)
    dma = pltpu.SemaphoreType.DMA
    messages = len(PAIRS)
    x, sol = pl.pallas_call(
        kernel,
        out_shape=(jax.ShapeDtypeStruct((512, 512), BF16), jax.ShapeDtypeStruct((6, 256, 128), F32)),
        in_specs=[anywhere, anywhere, anywhere, scalars, scalars, anywhere, anywhere, anywhere],
        out_specs=(vmem, vmem),
        scratch_shapes=[
            pltpu.VMEM((512, 512), BF16),
            pltpu.VMEM((4, 512, 512), BF16),
            pltpu.VMEM((768, 512), BF16),
            pltpu.VMEM((6, 256, 256), F32),
            pltpu.VMEM((5, 256, 256), F32),
            pltpu.VMEM((6, 256, 128), F32),
            pltpu.VMEM((512, 512), BF16),
            pltpu.VMEM((4, 2, 256, 512), F32),
            pltpu.VMEM((3, 2, 256, 512), BF16),
            pltpu.VMEM((5, 256, 512), BF16),
            pltpu.VMEM((4, 2, 256, 512), BF16),
            pltpu.VMEM((4, 2, 64, 768), F32),
            pltpu.VMEM((4, 2, 64, 768), BF16),
            pltpu.VMEM((2, 64, 768), BF16),
            pltpu.VMEM((2, 64, 768), BF16),
            pltpu.VMEM((2, 2, 64, 768), BF16),
            pltpu.VMEM((64, 768), BF16),
            pltpu.VMEM((16, 256), F32),
            pltpu.VMEM((16, 256), F32),
            pltpu.VMEM((6, 512, 256), BF16),
            pltpu.VMEM((6, 512, 768), BF16),
            pltpu.VMEM((6, 768, 256), BF16),
            pltpu.VMEM((6, 768, 256), BF16),
            pltpu.VMEM((6, 128, 256), F32),
            pltpu.VMEM((6, 64, 256), F32),
            pltpu.VMEM((6, 64, 256), F32),
            pltpu.VMEM((6, 64, 256), F32),
            pltpu.VMEM((messages, 64, 256), HOP),
            pltpu.VMEM((messages, 64, 256), HOP),
            pltpu.VMEM((6, 128, 256), F32),
            pltpu.VMEM((64, 768), BF16),
            pltpu.VMEM((8, 64, 768), BF16),
            pltpu.VMEM((4, 2, 256, 512), BF16),
            pltpu.VMEM((2, 256, 512), F32),
            dma((9,)),
            dma((6,)),
            dma((5,)),
            dma((7,)),
            dma((3,)),
            dma((2, 2)),
            dma,
            dma,
            dma((messages,)),
            dma((messages,)),
            dma,
            dma,
            dma((7,)),
            dma((8,)),
            dma((5,)),
            dma((4, 2)),
        ],
        compiler_params=pltpu.CompilerParams(
            collective_id=0, has_side_effects=True, vmem_limit_bytes=60 * 1024 * 1024
        ),
    )(
        leaf_rhs[0],
        leaf_inverse[0],
        panels[0].reshape(768, 512),
        pattern,
        offsets,
        sep_inverse[0],
        sep_link[0],
        sep_rhs[0],
    )
    return x[None], sol[None]


def solution(mesh):
    in_specs = (
        P("leaf", "col", None),
        P("leaf", None, "col"),
        P("leaf", None, None, "col"),
        P("leaf", None),
        P("leaf", None),
        P("leaf", None, None, None),
        P("leaf", None, None, None),
        P("leaf", None, None, None),
    )
    out_specs = (P("leaf", "col", None), P("leaf", None, None, "col"))
    return jax.shard_map(on_device, mesh=mesh, in_specs=in_specs, out_specs=out_specs, check_vma=False)
```

time: 265 us -> 98.9 us (0.37)
  the two profiles are of different devices: /device:TPU:102 before, /device:TPU:1 now
where the time goes in v1:
time: 98.9 us; the launch traced here: 98.7 us
  Pallas kernels  94.1 us (95%)
  local copies, waits for them, and re-layouts  3.93 us (4%)
    pallas_call x1, Pallas kernels, on_device(): pl.pallas_call(kernel, out_shape=(jax.ShapeDtypeStruct((512, 512), BF16),...  94.1 us
    unnamed x2, local copies, waits for them, and re-layouts  3.93 us

profile of v1, /device:TPU:1, one launch (start us, length us, event | category | flops | bytes accessed | tf_op | source)
XLA Modules:
  0.0 98.7 jit_solution(2112167735506094670)
XLA Ops:
  0.6 94.1 %shard_map.95 = (bf16[512,512]{1,0:T(8,128)(2,1)}, f32[6,256,128]{2,1,0:T(8,128)}) custom-call(bf16[512,512]{1,0:T(8,128)(2,1)} %bitcast.14, bf16[2048,512]{1,0:T(8,128)(2,1)} %bitcast.9, bf16[768,512]{1,0:T(8,128)(2,1)} %bitcast.12, s32[1,6]{1,0:T(1,128)} %pat.1, s32[1,6]{1,0:T(1,128)} %off.1, f32[6,256,256]{2,1,0:T(8,128)} %bitcast.10, ...), custom_call_target="tpu_custom_call" | custom-call | tf_op jit(solution)/shard_map/pallas_call | solution.py:388
  94.8 1.9 %copy.12 = bf16[1,512,512]{2,1,0:T(8,128)(2,1)} copy(bf16[1,512,512]{2,1,0:T(8,128)(2,1)} %bitcast.15) | data formatting | bytes 1048576
  96.6 2.1 %copy.13 = f32[1,6,256,128]{3,2,1,0:T(8,128)} copy(f32[1,6,256,128]{3,2,1,0:T(8,128)} %bitcast.13) | data formatting | bytes 1572864

commit v2 on v1

--- a/solution.py
+++ b/solution.py
@@ -36,10 +36,10 @@
 
 def kernel(
     rhs, inv, pan, pat, off, sinv, slink, srhs, x_out, sol_out,
-    rhs_v, inv_v, pan_v, sinv_v, slink_v, srhs_v,
-    bt, fp, fsnd, frx, sol_v, cc, cb, prl, psum, prx, pon, meta, metarx, est,
-    wf, wi, wg, rt, u, fs, bs, tsnd, trx, ball, soth, sall, redv, xacc,
-    ld, f_ss, f_rs, p_ss, p_rs, prx_rs, m_ss, m_rs, t_ss, t_rs, b_ss, b_rs, s_ss, s_rs, r_ss, r_rs,
+    rhs_v, inv_v, big, sinv_v, slink_v, srhs_v,
+    bt, fp, fsnd, frx, cc, cb, prl, psum, prx, pon, meta, metarx, est,
+    wf, wi, wg, rt, u, fs, bs, tsnd, trx, ball, solt, soth, sall, acc, xt,
+    ld, f_ss, f_rs, p_ss, p_rs, prx_rs, m_ss, m_rs, t_ss, t_rs, b_ss, b_rs, s_ss, s_rs, g_ss, g_rs, o_s,
 ):
     leaf = lax.axis_index("leaf")
     c = lax.axis_index("col")
@@ -71,7 +71,7 @@
             pltpu.make_async_copy(inv.at[pl.ds(pl.multiple_of(r * rows, rows), rows)], inv_v.at[r], ld.at[1 + step])
         )
         on(step <= 3 - c, load_inv[step].start)
-    load_pan = pltpu.make_async_copy(pan, pan_v, ld.at[5])
+    load_pan = pltpu.make_async_copy(pan, big.at[c, pl.ds(0, 3)], ld.at[5])
     load_pan.start()
     load_sinv = pltpu.make_async_copy(sinv, sinv_v, ld.at[6])
     load_sinv.start()
@@ -141,6 +141,34 @@
 
         on(step <= 3 - c, block)
 
+    load_pan.wait()
+    flows = []
+
+    def flow(sender, number, r, p, to_col):
+        copy = remote(big.at[r, p], big.at[r, p], g_ss.at[number], g_rs.at[r, p], leaf, to_col)
+        flows.append((c == sender, copy))
+        return flows[-1]
+
+    def arrive(r, p):
+        remote(big.at[r, p], big.at[r, p], g_ss.at[0], g_rs.at[r, p], leaf, c1).wait_recv()
+
+    def start(*items):
+        for cond, copy in items:
+            on(cond, copy.start)
+
+    def forward(cond, steps):
+        def run():
+            for r, p, (_, copy) in steps:
+                arrive(r, p)
+                copy.start()
+
+        on(cond, run)
+
+    start(*(flow(3, p, 3, p, 0) for p in range(3)), flow(3, 3, 3, 0, 2))
+    start(*(flow(2, p, 2, p, 1) for p in range(3)), flow(2, 3, 2, 2, 3))
+    start(flow(1, 0, 1, 0, 0))
+    second = flow(3, 4, 3, 1, 2)
+
     load_sinv.wait()
     load_slink.wait()
     load_srhs.wait()
@@ -179,6 +207,9 @@
             est[k, pl.ds(part * 256, 128), :] = hot
             est[k, pl.ds(part * 256 + 128, 128), :] = hot
 
+    def product(r, p):
+        return dot_nn(big[r, p], inv_v[r])
+
     def frecv(slot, from_col):
         remote(frx.at[slot], frx.at[slot], f_ss.at[0], f_rs.at[slot], leaf, from_col).wait_recv()
 
@@ -188,7 +219,7 @@
             fsnd[2, h] = (fp[2, h] + frx[h].astype(F32)).astype(BF16)
             msgs[name][1].start()
         for h in range(2):
-            sol_v[0, h] = fp[3, h].astype(BF16)
+            big[0, 3 + h] = fp[3, h].astype(BF16)
 
     def after1():
         frecv(0, 0)
@@ -196,30 +227,30 @@
         msgs["21A"][1].start()
         for h in range(2):
             frecv(1 + h, 0)
-            sol_v[1, h] = (fp[2, h] + frx[1 + h].astype(F32)).astype(BF16)
+            big[1, 3 + h] = (fp[2, h] + frx[1 + h].astype(F32)).astype(BF16)
 
     def after2():
         frecv(1, 1)
-        sol_v[2, 0] = (fp[1, 0] + frx[1].astype(F32)).astype(BF16)
+        big[2, 3] = (fp[1, 0] + frx[1].astype(F32)).astype(BF16)
         frecv(0, 1)
         frecv(2, 3)
-        sol_v[2, 1] = (fp[1, 1] + frx[0].astype(F32) + frx[2].astype(F32)).astype(BF16)
+        big[2, 4] = (fp[1, 1] + frx[0].astype(F32) + frx[2].astype(F32)).astype(BF16)
 
     def after3():
         frecv(0, 0)
         msgs["relay"][1].start()
+        second[1].start()
         for h in range(2):
             frecv(3 + h, 2)
             frecv(1 + h, 0)
-            sol_v[3, h] = (fp[0, h] + frx[1 + h].astype(F32) + frx[3 + h].astype(F32)).astype(BF16)
+            big[3, 3 + h] = (fp[0, h] + frx[1 + h].astype(F32) + frx[3 + h].astype(F32)).astype(BF16)
 
     for group, fn in enumerate((after0, after1, after2, after3)):
         on(c == group, fn)
 
-    load_pan.wait()
-    panels = pan_v
+    panels = big[c, pl.ds(0, 3)].reshape(768, 512)
     for h in range(2):
-        share = dot_nt(sol_v[c, h], panels[...]).reshape(2, 2, 64, 768)
+        share = dot_nt(big[c, 3 + h], panels).reshape(2, 2, 64, 768)
         cc[pl.ds(2 * h, 2)] = share
         cb[pl.ds(2 * h, 2)] = share.astype(BF16)
     relay_up = remote(cb.at[c2, 0], prl.at[0], p_ss.at[0], p_rs.at[0], leaf, c1)
@@ -237,6 +268,13 @@
     relay_down.wait_recv()
     psum[1] = (cc[c3, 1] + prl[1].astype(F32)).astype(BF16)
     sum_down.start()
+    start(flow(3, 5, 3, 3, 0), flow(3, 6, 3, 4, 0), flow(3, 7, 3, 2, 2), flow(3, 8, 3, 3, 2), flow(3, 9, 3, 4, 2))
+    start(flow(2, 4, 2, 3, 1), flow(2, 5, 2, 4, 1), flow(2, 6, 2, 3, 3), flow(2, 7, 2, 4, 3))
+    start(flow(1, 1, 1, 1, 0), flow(1, 2, 1, 2, 0), flow(1, 3, 1, 3, 0), flow(1, 4, 1, 4, 0))
+    forward(c == 3, [(2, 2, flow(3, 10, 2, 2, 0))])
+    forward(c == 2, [(3, 0, flow(2, 8, 3, 0, 1)), (3, 1, flow(2, 9, 3, 1, 1))])
+    forward(c == 1, [(2, 0, flow(1, 5, 2, 0, 0)), (2, 1, flow(1, 6, 2, 1, 0))])
+    forward(c == 0, [(3, 2, flow(0, 0, 3, 2, 1))])
     across.wait_recv()
 
     def precv(p, d, from_col):
@@ -282,6 +320,12 @@
                     receive(k, j)
                 send(k + 1, j)
         fs[k] = dot_nn(wide(both[:, :256]), wi[k])
+        if k < 5:
+            acc[k] = product(c, k)
+        if k == 3:
+            forward(c == 3, [(2, 3, flow(3, 11, 2, 3, 0)), (2, 4, flow(3, 12, 2, 4, 0))])
+            forward(c == 2, [(3, 3, flow(2, 10, 3, 3, 1))])
+            forward(c == 0, [(3, 4, flow(0, 1, 3, 4, 1))])
     for k in reversed(range(LEVELS)):
         down = fs[k]
         if k + 1 < LEVELS:
@@ -322,78 +366,60 @@
     theirs_rows = pl.ds(pl.multiple_of((1 - q) * 64, 64), 64)
     remote(ball.at[:, theirs_rows, :], ball.at[:, theirs_rows, :], b_ss, b_rs, other, c).wait_recv()
     for k in range(LEVELS):
-        sol_out[k] = ball[k].T
+        solt[k] = ball[k].T
+    put_sol = pltpu.make_async_copy(solt, sol_out, o_s.at[0])
+    put_sol.start()
+
+    for step in range(1, 4):
+
+        def add(step=step):
+            r = c + step
+            for p in range(5):
+                taken = (c == 0) & (r == 3) & (p in (2, 4))
+                taken |= (c == 1) & (r == 2) & (p in (0, 1))
+                taken |= (c == 2) & (r == 3) & (p in (0, 1, 3))
+                on(jnp.logical_not(taken), functools.partial(arrive, r, p))
+                acc[p] += product(r, p)
+
+        on(c + step <= 3, add)
 
     srecv(c * 2 + 1 - q, other, c)
     for p in range(2):
         srecv(far * 2 + p, base + p, far)
     for p in range(2):
         srecv(c2 * 2 + p, leaf, near)
-
+    weights = acc[pl.ds(0, 3)].reshape(768, 512).astype(BF16)
     for h in range(2):
         taken = sall[pl.ds(4 * h, 4)].reshape(256, 768)
-        redv[c, h] = (sol_v[c, h].astype(F32) - dot_nn(taken, panels[...])).astype(BF16)
-
-    def rmsg(sender, number, r, h, to_col):
-        return (c == sender, remote(redv.at[r, h], redv.at[r, h], r_ss.at[number], r_rs.at[r, h], leaf, to_col))
-
-    rfirst = [
-        rmsg(3, 0, 3, 1, 0), rmsg(3, 1, 3, 0, 0), rmsg(3, 2, 3, 0, 2), rmsg(3, 3, 3, 1, 2),
-        rmsg(2, 0, 2, 1, 3), rmsg(2, 1, 2, 0, 1), rmsg(2, 2, 2, 1, 1),
-        rmsg(1, 0, 1, 0, 0), rmsg(1, 1, 1, 1, 0),
-    ]
-    rnext = [rmsg(3, 4, 2, 1, 0), rmsg(2, 3, 3, 0, 1), rmsg(1, 2, 2, 0, 0), rmsg(0, 0, 3, 1, 1)]
-    for cond, copy in rfirst:
-        on(cond, copy.start)
-    for h in range(2):
-        xacc[h] = dot_nn(redv[c, h], inv_v[c])
-
-    def rrecv(r, h):
-        remote(redv.at[r, h], redv.at[r, h], r_ss.at[0], r_rs.at[r, h], leaf, c1).wait_recv()
-
-    for (cond, copy), (r, h) in zip(rnext, ((2, 1), (3, 0), (2, 0), (3, 1))):
-
-        def pass_on(copy=copy, r=r, h=h):
-            rrecv(r, h)
-            copy.start()
-
-        on(cond, pass_on)
-    for step in range(1, 4):
-
-        def add(step=step):
-            r = c + step
-            for h in range(2):
-                taken = ((c == 2) & (r == 3) & (h == 0)) | ((c == 1) & (r == 2) & (h == 0)) | ((c == 0) & (r == 3) & (h == 1))
-                on(jnp.logical_not(taken), functools.partial(rrecv, r, h))
-                xacc[h] += dot_nn(redv[r, h], inv_v[r])
-
-        on(c + step <= 3, add)
-    for h in range(2):
-        x_out[:, pl.ds(h * 256, 256)] = xacc[h].T.astype(BF16)
+        xt[:, pl.ds(h * 256, 256)] = (acc[3 + h] - dot_nn(taken, weights)).T.astype(BF16)
+    put_x = pltpu.make_async_copy(xt, x_out, o_s.at[1])
+    put_x.start()
 
     for copy in (send_meta, relay_up, relay_down, direct_up, direct_down, across, sum_up, sum_down, *s_copies, *relays):
         copy.wait_send()
     for k, j in PAIRS:
         tree(k, j).wait_send()
-    for cond, copy in (*msgs.values(), *rfirst, *rnext):
+    for cond, copy in (*msgs.values(), *flows):
         on(cond, copy.wait_send)
+    put_sol.wait()
+    put_x.wait()
 
 
 def on_device(leaf_rhs, leaf_inverse, panels, pattern, offsets, sep_inverse, sep_link, sep_rhs):
     anywhere = pl.BlockSpec(memory_space=pl.ANY)
+    hbm = pl.BlockSpec(memory_space=pltpu.HBM)
     scalars = pl.BlockSpec(memory_space=pltpu.SMEM)
-    vmem = pl.BlockSpec(memory_space=pltpu.VMEM)
     dma = pltpu.SemaphoreType.DMA
     messages = len(PAIRS)
     x, sol = pl.pallas_call(
         kernel,
         out_shape=(jax.ShapeDtypeStruct((512, 512), BF16), jax.ShapeDtypeStruct((6, 256, 128), F32)),
-        in_specs=[anywhere, anywhere, anywhere, scalars, scalars, anywhere, anywhere, anywhere],
-        out_specs=(vmem, vmem),
+        in_specs=[hbm, hbm, hbm, scalars, scalars, hbm, hbm, hbm],
+        out_specs=(anywhere, anywhere),
         scratch_shapes=[
             pltpu.VMEM((512, 512), BF16),
             pltpu.VMEM((4, 512, 512), BF16),
-            pltpu.VMEM((768, 512), BF16),
+            pltpu.VMEM((4, 5, 256, 512), BF16),
             pltpu.VMEM((6, 256, 256), F32),
             pltpu.VMEM((5, 256, 256), F32),
             pltpu.VMEM((6, 256, 128), F32),
@@ -401,7 +427,6 @@
             pltpu.VMEM((4, 2, 256, 512), F32),
             pltpu.VMEM((3, 2, 256, 512), BF16),
             pltpu.VMEM((5, 256, 512), BF16),
-            pltpu.VMEM((4, 2, 256, 512), BF16),
             pltpu.VMEM((4, 2, 64, 768), F32),
             pltpu.VMEM((4, 2, 64, 768), BF16),
             pltpu.VMEM((2, 64, 768), BF16),
@@ -421,10 +446,11 @@
             pltpu.VMEM((messages, 64, 256), HOP),
             pltpu.VMEM((messages, 64, 256), HOP),
             pltpu.VMEM((6, 128, 256), F32),
+            pltpu.VMEM((6, 256, 128), F32),
             pltpu.VMEM((64, 768), BF16),
             pltpu.VMEM((8, 64, 768), BF16),
-            pltpu.VMEM((4, 2, 256, 512), BF16),
-            pltpu.VMEM((2, 256, 512), F32),
+            pltpu.VMEM((5, 256, 512), F32),
+            pltpu.VMEM((512, 512), BF16),
             dma((9,)),
             dma((6,)),
             dma((5,)),
@@ -439,16 +465,17 @@
             dma,
             dma((7,)),
             dma((8,)),
-            dma((5,)),
-            dma((4, 2)),
+            dma((13,)),
+            dma((4, 5)),
+            dma((2,)),
         ],
         compiler_params=pltpu.CompilerParams(
-            collective_id=0, has_side_effects=True, vmem_limit_bytes=60 * 1024 * 1024
+            collective_id=0, has_side_effects=True, vmem_limit_bytes=46 * 1024 * 1024
         ),
     )(
         leaf_rhs[0],
         leaf_inverse[0],
-        panels[0].reshape(768, 512),
+        panels[0].reshape(3, 256, 512),
         pattern,
         offsets,
         sep_inverse[0],

time: 98.9 us -> 91.5 us (0.925)
  Pallas kernels: 94.1 us -> 81.1 us
  local copies, waits for them, and re-layouts: 3.93 us -> 9.47 us
    pallas_call x1, Pallas kernels: 94.1 us -> 81.1 us  [on_device(): pl.pallas_call(kernel, out_shape=(jax.ShapeDtypeStruct((512, 512), BF16),...]
    unnamed x2 -> x16, local copies, waits for them, and re-layouts: 3.93 us -> 9.47 us
where the time goes in v2:
time: 91.5 us; the launch traced here: 91.2 us
  Pallas kernels  81.1 us (89%)
  local copies, waits for them, and re-layouts  9.47 us (10%)
    pallas_call x1, Pallas kernels, on_device(): pl.pallas_call(kernel, out_shape=(jax.ShapeDtypeStruct((512, 512), BF16),...  81.1 us
    unnamed x16, local copies, waits for them, and re-layouts  9.47 us

profile of v2, /device:TPU:1, one launch (start us, length us, event | category | flops | bytes accessed | tf_op | source)
XLA Modules:
  0.0 91.2 jit_solution(13543424129200701807)
XLA Ops:
  0.6 0.0 copy-start
  0.6 1.6 %copy-done = bf16[1,2048,512]{2,1,0:T(8,128)(2,1)S(1)} copy-done((bf16[1,2048,512]{2,1,0:T(8,128)(2,1)S(1)}, bf16[1,2048,512]{2,1,0:T(8,128)(2,1)}, u32[]{:S(2)}) %copy-start) | copy-done | bytes 2097176
  2.2 0.0 copy-start.1
  2.2 1.4 %copy-done.1 = f32[1,6,256,256]{3,2,1,0:T(8,128)S(1)} copy-done((f32[1,6,256,256]{3,2,1,0:T(8,128)S(1)}, f32[1,6,256,256]{3,2,1,0:T(8,128)}, u32[]{:S(2)}) %copy-start.1) | copy-done | bytes 1572888
  3.6 0.0 copy-start.2
  3.6 1.3 %copy-done.2 = f32[1,5,256,256]{3,2,1,0:T(8,128)S(1)} copy-done((f32[1,5,256,256]{3,2,1,0:T(8,128)S(1)}, f32[1,5,256,256]{3,2,1,0:T(8,128)}, u32[]{:S(2)}) %copy-start.2) | copy-done | bytes 1310744
  5.0 0.0 copy-start.3
  5.0 1.1 %copy-done.3 = bf16[1,6,128,512]{3,2,1,0:T(8,128)(2,1)S(1)} copy-done((bf16[1,6,128,512]{3,2,1,0:T(8,128)(2,1)S(1)}, bf16[1,6,128,512]{3,2,1,0:T(8,128)(2,1)}, u32[]{:S(2)}) %copy-start.3) | copy-done | bytes 786456
  6.1 0.0 copy-start.4
  6.1 1.0 %copy-done.4 = bf16[1,512,512]{2,1,0:T(8,128)(2,1)S(1)} copy-done((bf16[1,512,512]{2,1,0:T(8,128)(2,1)S(1)}, bf16[1,512,512]{2,1,0:T(8,128)(2,1)}, u32[]{:S(2)}) %copy-start.4) | copy-done | bytes 524312
  7.1 0.0 copy-start.5
  7.1 0.7 copy-done.5
  7.8 0.0 copy-start.6
  7.8 0.7 copy-done.6
  8.4 81.1 %shard_map.95 = (bf16[512,512]{1,0:T(8,128)(2,1)S(1)}, f32[6,256,128]{2,1,0:T(8,128)S(1)}) custom-call(bf16[512,512]{1,0:T(8,128)(2,1)S(1)} %bitcast.13, bf16[2048,512]{1,0:T(8,128)(2,1)S(1)} %bitcast.8, bf16[3,256,512]{2,1,0:T(8,128)(2,1)S(1)} %bitcast.11, s32[1,6]{1,0:T(1,128)S(1)} %copy-done.5, s32[1,6]{1,0:T(1,128)S(1)} %copy-done.6, ...), custom_call_target="tpu_custom_call" | custom-call | tf_op jit(solution)/shard_map/pallas_call | solution.py:414
  89.5 0.8 copy.12
  90.3 0.9 copy.13
Async XLA Ops:
  0.6 1.6 %copy-start = (bf16[1,2048,512]{2,1,0:T(8,128)(2,1)S(1)}, bf16[1,2048,512]{2,1,0:T(8,128)(2,1)}, u32[]{:S(2)}) copy-start(bf16[1,2048,512]{2,1,0:T(8,128)(2,1)} %param.9) | copy-start | bytes 6291460
  2.2 1.4 %copy-start.1 = (f32[1,6,256,256]{3,2,1,0:T(8,128)S(1)}, f32[1,6,256,256]{3,2,1,0:T(8,128)}, u32[]{:S(2)}) copy-start(f32[1,6,256,256]{3,2,1,0:T(8,128)} %param.13) | copy-start | bytes 4718596
  3.6 1.3 %copy-start.2 = (f32[1,5,256,256]{3,2,1,0:T(8,128)S(1)}, f32[1,5,256,256]{3,2,1,0:T(8,128)}, u32[]{:S(2)}) copy-start(f32[1,5,256,256]{3,2,1,0:T(8,128)} %param.14) | copy-start | bytes 3932164
  5.0 1.1 %copy-start.3 = (bf16[1,6,128,512]{3,2,1,0:T(8,128)(2,1)S(1)}, bf16[1,6,128,512]{3,2,1,0:T(8,128)(2,1)}, u32[]{:S(2)}) copy-start(bf16[1,6,128,512]{3,2,1,0:T(8,128)(2,1)} %param.10) | copy-start | bytes 2359300
  6.1 1.0 %copy-start.4 = (bf16[1,512,512]{2,1,0:T(8,128)(2,1)S(1)}, bf16[1,512,512]{2,1,0:T(8,128)(2,1)}, u32[]{:S(2)}) copy-start(bf16[1,512,512]{2,1,0:T(8,128)(2,1)} %param.8) | copy-start | bytes 1572868
  7.1 0.7 copy-start.5
  7.8 0.7 copy-start.6

commit v3 on v2

--- a/solution.py
+++ b/solution.py
@@ -71,17 +71,6 @@
             pltpu.make_async_copy(inv.at[pl.ds(pl.multiple_of(r * rows, rows), rows)], inv_v.at[r], ld.at[1 + step])
         )
         on(step <= 3 - c, load_inv[step].start)
-    load_pan = pltpu.make_async_copy(pan, big.at[c, pl.ds(0, 3)], ld.at[5])
-    load_pan.start()
-    load_sinv = pltpu.make_async_copy(sinv, sinv_v, ld.at[6])
-    load_sinv.start()
-    load_slink = pltpu.make_async_copy(slink, slink_v, ld.at[7])
-    load_slink.start()
-    load_srhs = pltpu.make_async_copy(
-        srhs.at[:, :, pl.ds(pl.multiple_of(c * 128, 128), 128)], srhs_v, ld.at[8]
-    )
-    load_srhs.start()
-
     peers = [(leaf, c1), (leaf, c2), (leaf, c3)]
     peers += [(base + 1 - q, cc_) for cc_ in (c, c1, c2, c3)]
     peers += [(leaf ^ MASKS[k], c) for k in range(1, LEVELS)]
@@ -104,42 +93,47 @@
     def fmsg(sender, number, src, slot, to_col):
         return (c == sender, remote(src, frx.at[slot], f_ss.at[number], f_rs.at[slot], leaf, to_col))
 
-    msgs = {
-        "20A": fmsg(0, 0, fsnd.at[0, 0], 0, 1),
-        "20B": fmsg(0, 1, fsnd.at[0, 1], 0, 3),
-        "10A": fmsg(0, 2, fsnd.at[1, 0], 1, 1),
-        "10B": fmsg(0, 3, fsnd.at[1, 1], 2, 1),
-        "30A": fmsg(0, 4, fsnd.at[2, 0], 1, 3),
-        "30B": fmsg(0, 5, fsnd.at[2, 1], 2, 3),
-        "31A": fmsg(1, 0, fsnd.at[0, 0], 0, 0),
-        "31B": fmsg(1, 1, fsnd.at[0, 1], 1, 0),
-        "21B": fmsg(1, 2, fsnd.at[1, 1], 0, 2),
-        "21A": fmsg(1, 3, fsnd.at[1, 0], 1, 2),
-        "32A": fmsg(2, 0, fsnd.at[0, 0], 3, 3),
-        "32B": fmsg(2, 1, fsnd.at[0, 1], 4, 3),
-        "relay": fmsg(3, 0, frx.at[0], 2, 2),
-    }
-    now = {
-        (0, 0): ("20A", "31A", "32A"),
-        (0, 1): ("20B", "31B", "32B"),
-        (1, 0): ("10A",),
-        (1, 1): ("10B", "21B"),
-    }
+    msgs = {}
+
+    def messages(sender, to_col, items):
+        for step, n, slot in items:
+            number = sum(1 for key in msgs if key[0] == sender)
+            msgs[sender, to_col, step, n] = fmsg(sender, number, fsnd.at[step, n], slot, to_col)
+
+    messages(0, 1, [(0, 0, 0), (0, 1, 1), (1, 0, 2), (1, 1, 3), (1, 2, 4), (1, 3, 5)])
+    messages(0, 3, [(0, 2, 0), (0, 3, 1), (2, 2, 4), (2, 3, 5), (2, 0, 2), (2, 1, 3)])
+    messages(1, 0, [(0, 0, 0), (0, 1, 1)])
+    messages(1, 2, [(0, 2, 0), (0, 3, 1), (1, 2, 4), (1, 3, 5), (1, 0, 2), (1, 1, 3)])
+    messages(2, 3, [(0, 0, 6), (0, 1, 7), (0, 2, 8), (0, 3, 9)])
+    msgs[3, 2, 9, 0] = fmsg(3, 0, frx.at[0], 6, 2)
+    msgs[3, 2, 9, 1] = fmsg(3, 1, frx.at[1], 7, 2)
+    later = {(0, 3, 2, 0), (0, 3, 2, 1), (1, 2, 1, 0), (1, 2, 1, 1), (2, 3, 0, 2), (2, 3, 0, 3)}
     for step in range(4):
 
         def block(step=step):
             load_inv[step].wait()
             r = order(step)
             for h in range(2):
-                value = dot_nt(bt[pl.ds(h * 256, 256), :], inv_v[r])
-                fp[step, h] = value
+                value = dot_nt(bt[pl.ds(h * 256, 256), :], inv_v[r]).reshape(2, 128, 512)
+                fp[step, pl.ds(2 * h, 2)] = value
                 if step < 3:
-                    fsnd[step, h] = value.astype(BF16)
-                for name in now.get((step, h), ()):
-                    cond, copy = msgs[name]
-                    on(cond, copy.start)
+                    fsnd[step, pl.ds(2 * h, 2)] = value.astype(BF16)
+                for key, (cond, copy) in msgs.items():
+                    if key[2] == step and key[3] // 2 == h and key not in later:
+                        on(cond, copy.start)
 
         on(step <= 3 - c, block)
+        if step == 0:
+            load_pan = pltpu.make_async_copy(pan, big.at[c, pl.ds(0, 3)], ld.at[5])
+            load_pan.start()
+            load_sinv = pltpu.make_async_copy(sinv, sinv_v, ld.at[6])
+            load_sinv.start()
+            load_slink = pltpu.make_async_copy(slink, slink_v, ld.at[7])
+            load_slink.start()
+            load_srhs = pltpu.make_async_copy(
+                srhs.at[:, :, pl.ds(pl.multiple_of(c * 128, 128), 128)], srhs_v, ld.at[8]
+            )
+            load_srhs.start()
 
     load_pan.wait()
     flows = []
@@ -166,7 +160,7 @@
 
     start(*(flow(3, p, 3, p, 0) for p in range(3)), flow(3, 3, 3, 0, 2))
     start(*(flow(2, p, 2, p, 1) for p in range(3)), flow(2, 3, 2, 2, 3))
-    start(flow(1, 0, 1, 0, 0))
+    start(flow(1, 0, 1, 0, 0), flow(1, 1, 1, 1, 0))
     second = flow(3, 4, 3, 1, 2)
 
     load_sinv.wait()
@@ -213,46 +207,57 @@
     def frecv(slot, from_col):
         remote(frx.at[slot], frx.at[slot], f_ss.at[0], f_rs.at[slot], leaf, from_col).wait_recv()
 
+    def got(slot, from_col):
+        frecv(slot, from_col)
+        return frx[slot].astype(F32)
+
+    def add_and_send(key, slot, from_col):
+        _, _, step, n = key
+        fsnd[step, n] = (fp[step, n] + got(slot, from_col)).astype(BF16)
+        msgs[key][1].start()
+
+    def solved(r, n, value):
+        big[r, 3 + n // 2, pl.ds(n % 2 * 128, 128), :] = value.astype(BF16)
+
     def after0():
-        for h, name in enumerate(("30A", "30B")):
-            frecv(h, 1)
-            fsnd[2, h] = (fp[2, h] + frx[h].astype(F32)).astype(BF16)
-            msgs[name][1].start()
-        for h in range(2):
-            big[0, 3 + h] = fp[3, h].astype(BF16)
+        add_and_send((0, 3, 2, 0), 0, 1)
+        add_and_send((0, 3, 2, 1), 1, 1)
+        for n in range(4):
+            solved(0, n, fp[3, n])
 
     def after1():
-        frecv(0, 0)
-        fsnd[1, 0] = (fp[1, 0] + frx[0].astype(F32)).astype(BF16)
-        msgs["21A"][1].start()
-        for h in range(2):
-            frecv(1 + h, 0)
-            big[1, 3 + h] = (fp[2, h] + frx[1 + h].astype(F32)).astype(BF16)
+        add_and_send((1, 2, 1, 0), 0, 0)
+        add_and_send((1, 2, 1, 1), 1, 0)
+        for n in range(4):
+            solved(1, n, fp[2, n] + got(2 + n, 0))
 
     def after2():
-        frecv(1, 1)
-        big[2, 3] = (fp[1, 0] + frx[1].astype(F32)).astype(BF16)
-        frecv(0, 1)
-        frecv(2, 3)
-        big[2, 4] = (fp[1, 1] + frx[0].astype(F32) + frx[2].astype(F32)).astype(BF16)
+        add_and_send((2, 3, 0, 2), 0, 1)
+        add_and_send((2, 3, 0, 3), 1, 1)
+        for n in (2, 3):
+            solved(2, n, fp[1, n] + got(2 + n, 1) + got(4 + n, 3))
+        for n in (0, 1):
+            solved(2, n, fp[1, n] + got(2 + n, 1))
 
     def after3():
-        frecv(0, 0)
-        msgs["relay"][1].start()
+        for n in range(2):
+            frecv(n, 0)
+            msgs[3, 2, 9, n][1].start()
         second[1].start()
-        for h in range(2):
-            frecv(3 + h, 2)
-            frecv(1 + h, 0)
-            big[3, 3 + h] = (fp[0, h] + frx[1 + h].astype(F32) + frx[3 + h].astype(F32)).astype(BF16)
+        for n in (2, 3, 0, 1):
+            solved(3, n, fp[0, n] + got(6 + n, 2) + got(2 + n, 0))
 
     for group, fn in enumerate((after0, after1, after2, after3)):
         on(c == group, fn)
 
     panels = big[c, pl.ds(0, 3)].reshape(768, 512)
-    for h in range(2):
-        share = dot_nt(big[c, 3 + h], panels).reshape(2, 2, 64, 768)
-        cc[pl.ds(2 * h, 2)] = share
-        cb[pl.ds(2 * h, 2)] = share.astype(BF16)
+
+    def share(j):
+        rows_j = pl.ds(pl.multiple_of(lax.rem(j, 2) * 128, 128), 128)
+        value = dot_nt(big[c, 3 + lax.div(j, 2), rows_j, :], panels).reshape(2, 64, 768)
+        cc[j] = value
+        cb[j] = value.astype(BF16)
+
     relay_up = remote(cb.at[c2, 0], prl.at[0], p_ss.at[0], p_rs.at[0], leaf, c1)
     relay_down = remote(cb.at[c2, 1], prl.at[1], p_ss.at[1], p_rs.at[1], leaf, c3)
     direct_up = remote(cb.at[c1, 1], prx.at[q, 0], p_ss.at[2], prx_rs.at[q, 0], base + 1, c1)
@@ -260,8 +265,15 @@
     across = remote(cb.at[c, 1 - q], pon, p_ss.at[4], p_rs.at[2], other, c)
     sum_up = remote(psum.at[0], prx.at[q, 0], p_ss.at[5], prx_rs.at[q, 0], base, c1)
     sum_down = remote(psum.at[1], prx.at[q, 1], p_ss.at[6], prx_rs.at[q, 1], base + 1, c3)
-    for copy in (relay_up, relay_down, direct_up, direct_down, across):
-        copy.start()
+    share(c2)
+    relay_up.start()
+    relay_down.start()
+    share(c1)
+    direct_up.start()
+    share(c3)
+    direct_down.start()
+    share(c)
+    across.start()
     relay_up.wait_recv()
     psum[0] = (cc[c1, 0] + prl[0].astype(F32)).astype(BF16)
     sum_up.start()
@@ -270,7 +282,7 @@
     sum_down.start()
     start(flow(3, 5, 3, 3, 0), flow(3, 6, 3, 4, 0), flow(3, 7, 3, 2, 2), flow(3, 8, 3, 3, 2), flow(3, 9, 3, 4, 2))
     start(flow(2, 4, 2, 3, 1), flow(2, 5, 2, 4, 1), flow(2, 6, 2, 3, 3), flow(2, 7, 2, 4, 3))
-    start(flow(1, 1, 1, 1, 0), flow(1, 2, 1, 2, 0), flow(1, 3, 1, 3, 0), flow(1, 4, 1, 4, 0))
+    start(flow(1, 2, 1, 2, 0), flow(1, 3, 1, 3, 0), flow(1, 4, 1, 4, 0))
     forward(c == 3, [(2, 2, flow(3, 10, 2, 2, 0))])
     forward(c == 2, [(3, 0, flow(2, 8, 3, 0, 1)), (3, 1, flow(2, 9, 3, 1, 1))])
     forward(c == 1, [(2, 0, flow(1, 5, 2, 0, 0)), (2, 1, flow(1, 6, 2, 1, 0))])
@@ -383,17 +395,27 @@
 
         on(c + step <= 3, add)
 
+    weights = acc[pl.ds(0, 3)].reshape(768, 512).astype(BF16)
+    puts = []
+
+    def final(y):
+        taken = sall[pl.ds(2 * y, 2)].reshape(128, 768)
+        rows_y = pl.ds(pl.multiple_of(lax.rem(y, 2) * 128, 128), 128)
+        to = pl.ds(pl.multiple_of(y * 128, 128), 128)
+        value = acc[3 + lax.div(y, 2), rows_y, :] - dot_nn(taken, weights)
+        xt[:, to] = value.T.astype(BF16)
+        puts.append(pltpu.make_async_copy(xt.at[:, to], x_out.at[:, to], o_s.at[1 + len(puts)]))
+        puts[-1].start()
+
     srecv(c * 2 + 1 - q, other, c)
+    final(c)
+    final(near)
     for p in range(2):
         srecv(far * 2 + p, base + p, far)
+    final(far)
     for p in range(2):
         srecv(c2 * 2 + p, leaf, near)
-    weights = acc[pl.ds(0, 3)].reshape(768, 512).astype(BF16)
-    for h in range(2):
-        taken = sall[pl.ds(4 * h, 4)].reshape(256, 768)
-        xt[:, pl.ds(h * 256, 256)] = (acc[3 + h] - dot_nn(taken, weights)).T.astype(BF16)
-    put_x = pltpu.make_async_copy(xt, x_out, o_s.at[1])
-    put_x.start()
+    final(c2)
 
     for copy in (send_meta, relay_up, relay_down, direct_up, direct_down, across, sum_up, sum_down, *s_copies, *relays):
         copy.wait_send()
@@ -402,11 +424,13 @@
     for cond, copy in (*msgs.values(), *flows):
         on(cond, copy.wait_send)
     put_sol.wait()
-    put_x.wait()
+    for put in puts:
+        put.wait()
 
 
 def on_device(leaf_rhs, leaf_inverse, panels, pattern, offsets, sep_inverse, sep_link, sep_rhs):
     anywhere = pl.BlockSpec(memory_space=pl.ANY)
+    in_hbm = functools.partial(pltpu.with_memory_space_constraint, memory_space=pltpu.HBM)
     hbm = pl.BlockSpec(memory_space=pltpu.HBM)
     scalars = pl.BlockSpec(memory_space=pltpu.SMEM)
     dma = pltpu.SemaphoreType.DMA
@@ -424,9 +448,9 @@
             pltpu.VMEM((5, 256, 256), F32),
             pltpu.VMEM((6, 256, 128), F32),
             pltpu.VMEM((512, 512), BF16),
-            pltpu.VMEM((4, 2, 256, 512), F32),
-            pltpu.VMEM((3, 2, 256, 512), BF16),
-            pltpu.VMEM((5, 256, 512), BF16),
+            pltpu.VMEM((4, 4, 128, 512), F32),
+            pltpu.VMEM((3, 4, 128, 512), BF16),
+            pltpu.VMEM((10, 128, 512), BF16),
             pltpu.VMEM((4, 2, 64, 768), F32),
             pltpu.VMEM((4, 2, 64, 768), BF16),
             pltpu.VMEM((2, 64, 768), BF16),
@@ -452,8 +476,8 @@
             pltpu.VMEM((5, 256, 512), F32),
             pltpu.VMEM((512, 512), BF16),
             dma((9,)),
-            dma((6,)),
-            dma((5,)),
+            dma((12,)),
+            dma((10,)),
             dma((7,)),
             dma((3,)),
             dma((2, 2)),
@@ -467,20 +491,20 @@
             dma((8,)),
             dma((13,)),
             dma((4, 5)),
-            dma((2,)),
+            dma((5,)),
         ],
         compiler_params=pltpu.CompilerParams(
             collective_id=0, has_side_effects=True, vmem_limit_bytes=46 * 1024 * 1024
         ),
     )(
-        leaf_rhs[0],
-        leaf_inverse[0],
-        panels[0].reshape(3, 256, 512),
-        pattern,
-        offsets,
-        sep_inverse[0],
-        sep_link[0],
-        sep_rhs[0],
+        in_hbm(leaf_rhs[0]),
+        in_hbm(leaf_inverse[0]),
+        in_hbm(panels[0].reshape(3, 256, 512)),
+        in_hbm(pattern),
+        in_hbm(offsets),
+        in_hbm(sep_inverse[0]),
+        in_hbm(sep_link[0]),
+        in_hbm(sep_rhs[0]),
     )
     return x[None], sol[None]
 

time: 91.5 us -> 78 us (0.85)
  local copies, waits for them, and re-layouts: 9.47 us -> 1.67 us
  Pallas kernels: 81.1 us -> 75.5 us
    unnamed x16 -> x2, local copies, waits for them, and re-layouts: 9.47 us -> 1.67 us
    pallas_call x1, Pallas kernels: 81.1 us -> 75.5 us  [on_device(): pl.pallas_call(kernel, out_shape=(jax.ShapeDtypeStruct((512, 512), BF16),...]
where the time goes in v3:
time: 78 us; the launch traced here: 77.9 us
  Pallas kernels  75.5 us (97%)
  local copies, waits for them, and re-layouts  1.67 us (2%)
    pallas_call x1, Pallas kernels, on_device(): pl.pallas_call(kernel, out_shape=(jax.ShapeDtypeStruct((512, 512), BF16),...  75.5 us
    unnamed x2, local copies, waits for them, and re-layouts  1.67 us

profile of v3, /device:TPU:1, one launch (start us, length us, event | category | flops | bytes accessed | tf_op | source)
XLA Modules:
  0.0 77.9 jit_solution(4706509561487025390)
XLA Ops:
  0.6 75.5 %shard_map.95 = (bf16[512,512]{1,0:T(8,128)(2,1)S(1)}, f32[6,256,128]{2,1,0:T(8,128)S(1)}) custom-call(bf16[512,512]{1,0:T(8,128)(2,1)} %bitcast.15, bf16[2048,512]{1,0:T(8,128)(2,1)} %bitcast.11, bf16[3,256,512]{2,1,0:T(8,128)(2,1)} %bitcast.14, s32[1,6]{1,0:T(1,128)} %pat.1, s32[1,6]{1,0:T(1,128)} %off.1, f32[6,256,256]{2,1,0:T(8,128)} %bitcast.12, ...), custom_call_target="tpu_custom_call" | custom-call | tf_op jit(solution)/shard_map/pallas_call | solution.py:438
  76.2 0.8 %copy.12 = bf16[1,512,512]{2,1,0:T(8,128)(2,1)} copy(bf16[1,512,512]{2,1,0:T(8,128)(2,1)S(1)} %bitcast.9) | data formatting | bytes 1048576
  77.0 0.9 %copy.13 = f32[1,6,256,128]{3,2,1,0:T(8,128)} copy(f32[1,6,256,128]{3,2,1,0:T(8,128)S(1)} %bitcast.8) | data formatting | bytes 1572864

commit v4 on v3

--- a/solution.py
+++ b/solution.py
@@ -174,13 +174,13 @@
         gk = lax.dot_general(
             slink_v[kk], ik, (((1,), (0,)), ((), ())), precision=highest, preferred_element_type=F32
         )
-        ih, il = halves(ik)
+        hk = lax.dot_general(ik, ik, (((0,), (0,)), ((), ())), precision=highest, preferred_element_type=F32)
         gh, gl = halves(gk)
-        for at, (hi, lo) in ((0, (ih, il)), (256, (gh, gl))):
-            wf[k, pl.ds(at, 256), pl.ds(0, 256)] = hi
-            wf[k, pl.ds(at, 256), pl.ds(256, 256)] = hi
-            wf[k, pl.ds(at, 256), pl.ds(512, 256)] = lo
-        for ref, (hi, lo) in ((wi, (ih, il)), (wg, (gh, gl))):
+        hh, hl = halves(hk)
+        wf[k, :, pl.ds(0, 256)] = gh
+        wf[k, :, pl.ds(256, 256)] = gh
+        wf[k, :, pl.ds(512, 256)] = gl
+        for ref, (hi, lo) in ((wi, (hh, hl)), (wg, (gh, gl))):
             ref[k, pl.ds(0, 256), :] = hi
             ref[k, pl.ds(256, 256), :] = hi
             ref[k, pl.ds(512, 256), :] = lo
@@ -321,58 +321,64 @@
     for k in range(LEVELS):
         if k > 0:
             receive(k, k)
-        both = dot_nt(wide(rt[k, mine_rows, :] - u[k]), wf[k])
+        right = wide(rt[k, mine_rows, :] - u[k])
         if k + 1 < LEVELS:
+            linked = dot_nt(right, wf[k])
             if k > 0:
                 receive(k, k + 1)
-            u[k + 1] = u[k + 1] + both[:, 256:]
+            u[k + 1] = u[k + 1] + linked
             send(k + 1, k + 1)
             for j in range(k + 2, LEVELS):
                 if k > 0:
                     receive(k, j)
                 send(k + 1, j)
-        fs[k] = dot_nn(wide(both[:, :256]), wi[k])
+        fs[k] = dot_nn(right, wi[k])
         if k < 5:
             acc[k] = product(c, k)
         if k == 3:
             forward(c == 3, [(2, 3, flow(3, 11, 2, 3, 0)), (2, 4, flow(3, 12, 2, 4, 0))])
             forward(c == 2, [(3, 3, flow(2, 10, 3, 3, 1))])
             forward(c == 0, [(3, 4, flow(0, 1, 3, 4, 1))])
-    for k in reversed(range(LEVELS)):
-        down = fs[k]
-        if k + 1 < LEVELS:
-            down = down - dot_nn(wide(bs[k + 1]), wg[k])
-        bs[k] = down
-        ball[k, mine_rows, :] = down
-
+    slot = c * 2 + q
+    near, far = jnp.where(q == 0, c3, c1), jnp.where(q == 0, c1, c3)
     swap = remote(ball.at[:, mine_rows, :], ball.at[:, mine_rows, :], b_ss, b_rs, other, c)
-    slot = c * 2 + q
-    for k in range(LEVELS):
-        low = bs[k].astype(BF16)
-        at = slice(k * 128, k * 128 + 128)
-        sall[slot, :, at] = dot_nt(low, est[k, pl.ds(0, 128), :]).astype(BF16)
-        soth[:, at] = dot_nt(low, est[k, pl.ds(256, 128), :]).astype(BF16)
-    s_copies = [
-        remote(sall.at[slot], sall.at[slot], s_ss.at[0], s_rs.at[slot], leaf, c1),
-        remote(soth, sall.at[slot], s_ss.at[1], s_rs.at[slot], other, c1),
-        remote(sall.at[slot], sall.at[slot], s_ss.at[2], s_rs.at[slot], leaf, c3),
-        remote(soth, sall.at[slot], s_ss.at[3], s_rs.at[slot], other, c3),
-        remote(soth, sall.at[slot], s_ss.at[4], s_rs.at[slot], other, c),
-    ]
-    for copy in s_copies:
-        copy.start()
+    s_copies = []
+
+    def block_of(ref, g):
+        return ref.at[:, pl.ds(256 * g, 256)]
+
+    for g in (2, 1, 0):
+        for k in (2 * g + 1, 2 * g):
+            down = fs[k]
+            if k + 1 < LEVELS:
+                down = down - dot_nn(wide(bs[k + 1]), wg[k])
+            bs[k] = down
+            ball[k, mine_rows, :] = down
+            low = down.astype(BF16)
+            at = slice(k * 128, k * 128 + 128)
+            sall[slot, :, at] = dot_nt(low, est[k, pl.ds(0, 128), :]).astype(BF16)
+            soth[:, at] = dot_nt(low, est[k, pl.ds(256, 128), :]).astype(BF16)
+        mine_g, to_g = block_of(sall.at[slot], g), block_of(sall.at[slot], g)
+        for n, (src, to_leaf, to_col) in enumerate(
+            ((mine_g, leaf, c1), (mine_g, leaf, c3), (block_of(soth, g), other, c1),
+             (block_of(soth, g), other, c3), (block_of(soth, g), other, c))
+        ):
+            s_copies.append(remote(src, to_g, s_ss.at[n, g], s_rs.at[slot, g], to_leaf, to_col))
+            s_copies[-1].start()
     swap.start()
 
-    def srecv(at, from_leaf, from_col):
-        remote(sall.at[at], sall.at[at], s_ss.at[0], s_rs.at[at], from_leaf, from_col).wait_recv()
-
-    near, far = jnp.where(q == 0, c3, c1), jnp.where(q == 0, c1, c3)
+    def srecv(at, g, from_leaf, from_col):
+        ref = block_of(sall.at[at], g)
+        remote(ref, ref, s_ss.at[0, g], s_rs.at[at, g], from_leaf, from_col).wait_recv()
+
     relays = []
-    for p in range(2):
-        at = near * 2 + p
-        srecv(at, base + p, near)
-        relays.append(remote(sall.at[at], sall.at[at], s_ss.at[5 + p], s_rs.at[at], leaf, far))
-        relays[p].start()
+    for g in (2, 1, 0):
+        for p in range(2):
+            at = near * 2 + p
+            srecv(at, g, base + p, near)
+            ref = block_of(sall.at[at], g)
+            relays.append(remote(ref, ref, s_ss.at[5 + p, g], s_rs.at[at, g], leaf, far))
+            relays[-1].start()
 
     remote(ball.at[:, mine_rows, :], ball.at[:, mine_rows, :], b_ss, b_rs, other, c).wait_send()
     theirs_rows = pl.ds(pl.multiple_of((1 - q) * 64, 64), 64)
@@ -407,14 +413,17 @@
         puts.append(pltpu.make_async_copy(xt.at[:, to], x_out.at[:, to], o_s.at[1 + len(puts)]))
         puts[-1].start()
 
-    srecv(c * 2 + 1 - q, other, c)
+    for g in range(3):
+        srecv(c * 2 + 1 - q, g, other, c)
     final(c)
     final(near)
     for p in range(2):
-        srecv(far * 2 + p, base + p, far)
+        for g in range(3):
+            srecv(far * 2 + p, g, base + p, far)
     final(far)
     for p in range(2):
-        srecv(c2 * 2 + p, leaf, near)
+        for g in range(3):
+            srecv(c2 * 2 + p, g, leaf, near)
     final(c2)
 
     for copy in (send_meta, relay_up, relay_down, direct_up, direct_down, across, sum_up, sum_down, *s_copies, *relays):
@@ -426,6 +435,14 @@
     put_sol.wait()
     for put in puts:
         put.wait()
+
+
+def write_out(x, sol, x_out, sol_out, sems):
+    copies = [pltpu.make_async_copy(x, x_out, sems.at[0]), pltpu.make_async_copy(sol, sol_out, sems.at[1])]
+    for copy in copies:
+        copy.start()
+    for copy in copies:
+        copy.wait()
 
 
 def on_device(leaf_rhs, leaf_inverse, panels, pattern, offsets, sep_inverse, sep_link, sep_rhs):
@@ -460,7 +477,7 @@
             pltpu.VMEM((16, 256), F32),
             pltpu.VMEM((16, 256), F32),
             pltpu.VMEM((6, 512, 256), BF16),
-            pltpu.VMEM((6, 512, 768), BF16),
+            pltpu.VMEM((6, 256, 768), BF16),
             pltpu.VMEM((6, 768, 256), BF16),
             pltpu.VMEM((6, 768, 256), BF16),
             pltpu.VMEM((6, 128, 256), F32),
@@ -487,8 +504,8 @@
             dma((messages,)),
             dma,
             dma,
-            dma((7,)),
-            dma((8,)),
+            dma((7, 3)),
+            dma((8, 3)),
             dma((13,)),
             dma((4, 5)),
             dma((5,)),
@@ -506,6 +523,14 @@
         in_hbm(sep_link[0]),
         in_hbm(sep_rhs[0]),
     )
+    x, sol = pl.pallas_call(
+        write_out,
+        out_shape=(jax.ShapeDtypeStruct((512, 512), BF16), jax.ShapeDtypeStruct((6, 256, 128), F32)),
+        in_specs=[anywhere, anywhere],
+        out_specs=(anywhere, anywhere),
+        scratch_shapes=[dma((2,))],
+        compiler_params=pltpu.CompilerParams(vmem_limit_bytes=1024 * 1024),
+    )(x, sol)
     return x[None], sol[None]
 
 

time: 78 us -> 77.3 us (level)
  local copies, waits for them, and re-layouts: 1.67 us -> 0 us
  Pallas kernels: 75.5 us -> 76.4 us
    unnamed x2 -> x0, local copies, waits for them, and re-layouts: 1.67 us -> none
    pallas_call x0 -> x1, Pallas kernels: none -> 1.07 us  [on_device(): pl.pallas_call(write_out, out_shape=(jax.ShapeDtypeStruct((512, 512), BF1...]
where the time goes in v4:
time: 77.3 us; the launch traced here: 77 us
  Pallas kernels  76.4 us (99%)
    pallas_call x1, Pallas kernels, on_device(): pl.pallas_call(kernel, out_shape=(jax.ShapeDtypeStruct((512, 512), BF16),...  75.3 us

profile of v4, /device:TPU:1, one launch (start us, length us, event | category | flops | bytes accessed | tf_op | source)
XLA Modules:
  0.0 77.0 jit_solution(16139155204190870945)
XLA Ops:
  0.6 75.3 %shard_map.95 = (bf16[512,512]{1,0:T(8,128)(2,1)S(1)}, f32[6,256,128]{2,1,0:T(8,128)S(1)}) custom-call(bf16[512,512]{1,0:T(8,128)(2,1)} %bitcast.13, bf16[2048,512]{1,0:T(8,128)(2,1)} %bitcast.9, bf16[3,256,512]{2,1,0:T(8,128)(2,1)} %bitcast.12, s32[1,6]{1,0:T(1,128)} %pat.1, s32[1,6]{1,0:T(1,128)} %off.1, f32[6,256,256]{2,1,0:T(8,128)} %bitcast.10, ...), custom_call_target="tpu_custom_call" | custom-call | tf_op jit(solution)/shard_map/pallas_call | solution.py:455
  76.0 1.1 %shard_map.96 = (bf16[512,512]{1,0:T(8,128)(2,1)}, f32[6,256,128]{2,1,0:T(8,128)}) custom-call(bf16[512,512]{1,0:T(8,128)(2,1)S(1)} %get-tuple-element.6.x, f32[6,256,128]{2,1,0:T(8,128)S(1)} %get-tuple-element.7.sol), custom_call_target="tpu_custom_call" | custom-call | tf_op jit(solution)/shard_map/pallas_call | solution.py:526

commit v5 on v4

--- a/solution.py
+++ b/solution.py
@@ -13,6 +13,12 @@
 HOP = BF16
 LEVELS = 6
 MASKS = (1, 2, 6, 8, 16, 56)
+PASSED = {0: {(3, 2), (3, 4)}, 1: {(2, 0), (2, 1)}, 2: {(3, 0), (3, 1), (3, 3)}}
+EARLY = {
+    0: {0: ((3, 0), (1, 0)), 1: ((3, 1), (1, 1)), 2: ((3, 2), (1, 2)), 3: ((3, 3),), 4: ((3, 4), (1, 3), (1, 4))},
+    1: {0: ((2, 0),), 1: ((2, 1),), 2: ((2, 2),), 4: ((2, 3), (2, 4))},
+    2: {4: ((3, 0), (3, 1))},
+}
 PAIRS = tuple((k, j) for k in range(1, LEVELS) for j in range(k, LEVELS))
 
 
@@ -339,6 +345,16 @@
             forward(c == 3, [(2, 3, flow(3, 11, 2, 3, 0)), (2, 4, flow(3, 12, 2, 4, 0))])
             forward(c == 2, [(3, 3, flow(2, 10, 3, 3, 1))])
             forward(c == 0, [(3, 4, flow(0, 1, 3, 4, 1))])
+        for group, windows in EARLY.items():
+            if k in windows:
+
+                def early(group=group, pieces=windows[k]):
+                    for r, p in pieces:
+                        if (r, p) not in PASSED[group]:
+                            arrive(r, p)
+                        acc[p] += product(r, p)
+
+                on(c == group, early)
     slot = c * 2 + q
     near, far = jnp.where(q == 0, c3, c1), jnp.where(q == 0, c1, c3)
     swap = remote(ball.at[:, mine_rows, :], ball.at[:, mine_rows, :], b_ss, b_rs, other, c)
@@ -388,18 +404,18 @@
     put_sol = pltpu.make_async_copy(solt, sol_out, o_s.at[0])
     put_sol.start()
 
-    for step in range(1, 4):
-
-        def add(step=step):
-            r = c + step
-            for p in range(5):
-                taken = (c == 0) & (r == 3) & (p in (2, 4))
-                taken |= (c == 1) & (r == 2) & (p in (0, 1))
-                taken |= (c == 2) & (r == 3) & (p in (0, 1, 3))
-                on(jnp.logical_not(taken), functools.partial(arrive, r, p))
-                acc[p] += product(r, p)
-
-        on(c + step <= 3, add)
+    for group in range(3):
+
+        def rest(group=group):
+            done = {piece for pieces in EARLY.get(group, {}).values() for piece in pieces}
+            for r in range(group + 1, 4):
+                for p in range(5):
+                    if (r, p) not in done:
+                        if (r, p) not in PASSED[group]:
+                            arrive(r, p)
+                        acc[p] += product(r, p)
+
+        on(c == group, rest)
 
     weights = acc[pl.ds(0, 3)].reshape(768, 512).astype(BF16)
     puts = []

time: 77.3 us -> 75.4 us (0.975)
  Pallas kernels: 76.4 us -> 74.2 us
    pallas_call x1, Pallas kernels: 75.3 us -> 73.2 us  [on_device(): pl.pallas_call(kernel, out_shape=(jax.ShapeDtypeStruct((512, 512), BF16),...]
where the time goes in v5:
time: 75.4 us; the launch traced here: 74.9 us
  Pallas kernels  74.2 us (98%)
    pallas_call x1, Pallas kernels, on_device(): pl.pallas_call(kernel, out_shape=(jax.ShapeDtypeStruct((512, 512), BF16),...  73.2 us

profile of v5, /device:TPU:1, one launch (start us, length us, event | category | flops | bytes accessed | tf_op | source)
XLA Modules:
  0.0 74.9 jit_solution(7439973904635880902)
XLA Ops:
  0.6 73.2 %shard_map.95 = (bf16[512,512]{1,0:T(8,128)(2,1)S(1)}, f32[6,256,128]{2,1,0:T(8,128)S(1)}) custom-call(bf16[512,512]{1,0:T(8,128)(2,1)} %bitcast.13, bf16[2048,512]{1,0:T(8,128)(2,1)} %bitcast.9, bf16[3,256,512]{2,1,0:T(8,128)(2,1)} %bitcast.12, s32[1,6]{1,0:T(1,128)} %pat.1, s32[1,6]{1,0:T(1,128)} %off.1, f32[6,256,256]{2,1,0:T(8,128)} %bitcast.10, ...), custom_call_target="tpu_custom_call" | custom-call | tf_op jit(solution)/shard_map/pallas_call | solution.py:471
  73.8 1.1 %shard_map.96 = (bf16[512,512]{1,0:T(8,128)(2,1)}, f32[6,256,128]{2,1,0:T(8,128)}) custom-call(bf16[512,512]{1,0:T(8,128)(2,1)S(1)} %get-tuple-element.6.x, f32[6,256,128]{2,1,0:T(8,128)S(1)} %get-tuple-element.7.sol), custom_call_target="tpu_custom_call" | custom-call | tf_op jit(solution)/shard_map/pallas_call | solution.py:542

commit v6 on v5

--- a/solution.py
+++ b/solution.py
@@ -12,13 +12,14 @@
 BF16 = jnp.bfloat16
 HOP = BF16
 LEVELS = 6
-MASKS = (1, 2, 6, 8, 16, 56)
-PASSED = {0: {(3, 2), (3, 4)}, 1: {(2, 0), (2, 1)}, 2: {(3, 0), (3, 1), (3, 3)}}
+MASKS = (1, 2, 6, 8, 16, 48)
+PASSED = {0: {(3, 1), (3, 2), (3, 4)}, 1: {(2, 0), (2, 1)}, 2: {(3, 0), (3, 3)}}
 EARLY = {
     0: {0: ((3, 0), (1, 0)), 1: ((3, 1), (1, 1)), 2: ((3, 2), (1, 2)), 3: ((3, 3),), 4: ((3, 4), (1, 3), (1, 4))},
-    1: {0: ((2, 0),), 1: ((2, 1),), 2: ((2, 2),), 4: ((2, 3), (2, 4))},
+    1: {0: ((2, 0),), 1: ((2, 1),), 2: ((2, 2),), 3: ((3, 1),), 4: ((3, 2), (2, 3), (2, 4))},
     2: {4: ((3, 0), (3, 1))},
 }
+NEXT = 56
 PAIRS = tuple((k, j) for k in range(1, LEVELS) for j in range(k, LEVELS))
 
 
@@ -80,21 +81,25 @@
     peers = [(leaf, c1), (leaf, c2), (leaf, c3)]
     peers += [(base + 1 - q, cc_) for cc_ in (c, c1, c2, c3)]
     peers += [(leaf ^ MASKS[k], c) for k in range(1, LEVELS)]
+    z = lax.div(leaf, 8)
+    sends_last = (z == 0) | (z == 3) | (z == 4) | (z == 7)
     barrier = pltpu.get_barrier_semaphore()
     for peer in peers:
         pl.semaphore_signal(barrier, inc=1, device_id=peer, device_id_type=MESH)
 
+    def greet_last():
+        pl.semaphore_signal(barrier, inc=1, device_id=(leaf ^ NEXT, c), device_id_type=MESH)
+
+    on(sends_last, greet_last)
+
     for k in range(LEVELS):
         meta[pl.ds(k, 1), :] = jnp.full((1, 256), off[0, k].astype(F32), F32)
         meta[pl.ds(8 + k, 1), :] = jnp.full((1, 256), pat[0, k].astype(F32), F32)
 
     load_rhs.wait()
     bt[...] = rhs_v[...].T
-    pl.semaphore_wait(barrier, len(peers))
-
     other = base + 1 - q
     send_meta = remote(meta, metarx, m_ss, m_rs, other, c)
-    send_meta.start()
 
     def fmsg(sender, number, src, slot, to_col):
         return (c == sender, remote(src, frx.at[slot], f_ss.at[number], f_rs.at[slot], leaf, to_col))
@@ -114,6 +119,12 @@
     msgs[3, 2, 9, 0] = fmsg(3, 0, frx.at[0], 6, 2)
     msgs[3, 2, 9, 1] = fmsg(3, 1, frx.at[1], 7, 2)
     later = {(0, 3, 2, 0), (0, 3, 2, 1), (1, 2, 1, 0), (1, 2, 1, 1), (2, 3, 0, 2), (2, 3, 0, 3)}
+
+    def go(step, h):
+        for key, (cond, copy) in msgs.items():
+            if key[2] == step and key[3] // 2 == h and key not in later:
+                on(cond, copy.start)
+
     for step in range(4):
 
         def block(step=step):
@@ -124,9 +135,8 @@
                 fp[step, pl.ds(2 * h, 2)] = value
                 if step < 3:
                     fsnd[step, pl.ds(2 * h, 2)] = value.astype(BF16)
-                for key, (cond, copy) in msgs.items():
-                    if key[2] == step and key[3] // 2 == h and key not in later:
-                        on(cond, copy.start)
+                if step > 0:
+                    go(step, h)
 
         on(step <= 3 - c, block)
         if step == 0:
@@ -140,6 +150,10 @@
                 srhs.at[:, :, pl.ds(pl.multiple_of(c * 128, 128), 128)], srhs_v, ld.at[8]
             )
             load_srhs.start()
+            pl.semaphore_wait(barrier, len(peers) + sends_last.astype(jnp.int32))
+            for h in range(2):
+                go(0, h)
+            send_meta.start()
 
     load_pan.wait()
     flows = []
@@ -290,9 +304,9 @@
     start(flow(2, 4, 2, 3, 1), flow(2, 5, 2, 4, 1), flow(2, 6, 2, 3, 3), flow(2, 7, 2, 4, 3))
     start(flow(1, 2, 1, 2, 0), flow(1, 3, 1, 3, 0), flow(1, 4, 1, 4, 0))
     forward(c == 3, [(2, 2, flow(3, 10, 2, 2, 0))])
-    forward(c == 2, [(3, 0, flow(2, 8, 3, 0, 1)), (3, 1, flow(2, 9, 3, 1, 1))])
+    forward(c == 2, [(3, 0, flow(2, 8, 3, 0, 1))])
     forward(c == 1, [(2, 0, flow(1, 5, 2, 0, 0)), (2, 1, flow(1, 6, 2, 1, 0))])
-    forward(c == 0, [(3, 2, flow(0, 0, 3, 2, 1))])
+    forward(c == 0, [(3, 1, flow(0, 0, 3, 1, 1)), (3, 2, flow(0, 1, 3, 2, 1))])
     across.wait_recv()
 
     def precv(p, d, from_col):
@@ -305,7 +319,8 @@
     theirs = pon[...].astype(F32) + prx[1 - q, 0].astype(F32) + prx[1 - q, 1].astype(F32)
     mh, ml = halves(mine)
     th, tl = halves(theirs)
-    for k in range(LEVELS):
+
+    def place(k):
         at = slice(k * 128, k * 128 + 128)
         left = jnp.concatenate([mh[:, at], ml[:, at], th[:, at], tl[:, at]], axis=1)
         u[k] = dot_nn(left, est[k])
@@ -316,14 +331,22 @@
         n = PAIRS.index((k, j))
         return remote(tsnd.at[n], trx.at[n], t_ss.at[n], t_rs.at[n], leaf ^ MASKS[k], c)
 
+    last = len(PAIRS) - 1
+    last_near = remote(tsnd.at[last], trx.at[last], t_ss.at[last + 1], t_rs.at[last], leaf ^ NEXT, c)
+
     def send(k, j):
         tsnd[PAIRS.index((k, j))] = u[j].astype(HOP)
-        tree(k, j).start()
+        if k + 1 < LEVELS:
+            tree(k, j).start()
+        else:
+            on(sends_last, last_near.start)
+            on(sends_last, tree(k, j).start)
 
     def receive(k, j):
         tree(k, j).wait_recv()
         u[j] = u[j] + trx[PAIRS.index((k, j))].astype(F32)
 
+    place(0)
     for k in range(LEVELS):
         if k > 0:
             receive(k, k)
@@ -332,19 +355,23 @@
             linked = dot_nt(right, wf[k])
             if k > 0:
                 receive(k, k + 1)
+            else:
+                place(1)
             u[k + 1] = u[k + 1] + linked
             send(k + 1, k + 1)
             for j in range(k + 2, LEVELS):
                 if k > 0:
                     receive(k, j)
+                else:
+                    place(j)
                 send(k + 1, j)
         fs[k] = dot_nn(right, wi[k])
         if k < 5:
             acc[k] = product(c, k)
         if k == 3:
             forward(c == 3, [(2, 3, flow(3, 11, 2, 3, 0)), (2, 4, flow(3, 12, 2, 4, 0))])
-            forward(c == 2, [(3, 3, flow(2, 10, 3, 3, 1))])
-            forward(c == 0, [(3, 4, flow(0, 1, 3, 4, 1))])
+            forward(c == 2, [(3, 3, flow(2, 9, 3, 3, 1))])
+            forward(c == 0, [(3, 4, flow(0, 2, 3, 4, 1))])
         for group, windows in EARLY.items():
             if k in windows:
 
@@ -444,8 +471,10 @@
 
     for copy in (send_meta, relay_up, relay_down, direct_up, direct_down, across, sum_up, sum_down, *s_copies, *relays):
         copy.wait_send()
-    for k, j in PAIRS:
+    for k, j in PAIRS[:-1]:
         tree(k, j).wait_send()
+    on(sends_last, tree(*PAIRS[-1]).wait_send)
+    on(sends_last, last_near.wait_send)
     for cond, copy in (*msgs.values(), *flows):
         on(cond, copy.wait_send)
     put_sol.wait()
@@ -516,7 +545,7 @@
             dma((2, 2)),
             dma,
             dma,
-            dma((messages,)),
+            dma((messages + 1,)),
             dma((messages,)),
             dma,
             dma,

time: 75.4 us -> 75.6 us (level)
  no operation moved by 1% of the time
where the time goes in v6:
time: 75.6 us; the launch traced here: 75.4 us
  Pallas kernels  74.8 us (99%)
    pallas_call x1, Pallas kernels, on_device(): pl.pallas_call(kernel, out_shape=(jax.ShapeDtypeStruct((512, 512), BF16),...  73.7 us

profile of v6, /device:TPU:1, one launch (start us, length us, event | category | flops | bytes accessed | tf_op | source)
XLA Modules:
  0.0 75.4 jit_solution(5646390508569116307)
XLA Ops:
  0.6 73.7 %shard_map.95 = (bf16[512,512]{1,0:T(8,128)(2,1)S(1)}, f32[6,256,128]{2,1,0:T(8,128)S(1)}) custom-call(bf16[512,512]{1,0:T(8,128)(2,1)} %bitcast.13, bf16[2048,512]{1,0:T(8,128)(2,1)} %bitcast.9, bf16[3,256,512]{2,1,0:T(8,128)(2,1)} %bitcast.12, s32[1,6]{1,0:T(1,128)} %pat.1, s32[1,6]{1,0:T(1,128)} %off.1, f32[6,256,256]{2,1,0:T(8,128)} %bitcast.10, ...), custom_call_target="tpu_custom_call" | custom-call | tf_op jit(solution)/shard_map/pallas_call | solution.py:500
  74.4 1.1 %shard_map.96 = (bf16[512,512]{1,0:T(8,128)(2,1)}, f32[6,256,128]{2,1,0:T(8,128)}) custom-call(bf16[512,512]{1,0:T(8,128)(2,1)S(1)} %get-tuple-element.6.x, f32[6,256,128]{2,1,0:T(8,128)S(1)} %get-tuple-element.7.sol), custom_call_target="tpu_custom_call" | custom-call | tf_op jit(solution)/shard_map/pallas_call | solution.py:571

commit v7 on v6

--- a/solution.py
+++ b/solution.py
@@ -180,7 +180,7 @@
 
     start(*(flow(3, p, 3, p, 0) for p in range(3)), flow(3, 3, 3, 0, 2))
     start(*(flow(2, p, 2, p, 1) for p in range(3)), flow(2, 3, 2, 2, 3))
-    start(flow(1, 0, 1, 0, 0), flow(1, 1, 1, 1, 0))
+    start(flow(1, 0, 1, 0, 0), flow(1, 1, 1, 1, 0), flow(1, 2, 1, 2, 0))
     second = flow(3, 4, 3, 1, 2)
 
     load_sinv.wait()
@@ -302,7 +302,7 @@
     sum_down.start()
     start(flow(3, 5, 3, 3, 0), flow(3, 6, 3, 4, 0), flow(3, 7, 3, 2, 2), flow(3, 8, 3, 3, 2), flow(3, 9, 3, 4, 2))
     start(flow(2, 4, 2, 3, 1), flow(2, 5, 2, 4, 1), flow(2, 6, 2, 3, 3), flow(2, 7, 2, 4, 3))
-    start(flow(1, 2, 1, 2, 0), flow(1, 3, 1, 3, 0), flow(1, 4, 1, 4, 0))
+    start(flow(1, 3, 1, 3, 0), flow(1, 4, 1, 4, 0))
     forward(c == 3, [(2, 2, flow(3, 10, 2, 2, 0))])
     forward(c == 2, [(3, 0, flow(2, 8, 3, 0, 1))])
     forward(c == 1, [(2, 0, flow(1, 5, 2, 0, 0)), (2, 1, flow(1, 6, 2, 1, 0))])
@@ -368,7 +368,7 @@
         fs[k] = dot_nn(right, wi[k])
         if k < 5:
             acc[k] = product(c, k)
-        if k == 3:
+        if k == 2:
             forward(c == 3, [(2, 3, flow(3, 11, 2, 3, 0)), (2, 4, flow(3, 12, 2, 4, 0))])
             forward(c == 2, [(3, 3, flow(2, 9, 3, 3, 1))])
             forward(c == 0, [(3, 4, flow(0, 2, 3, 4, 1))])

time: 75.6 us -> 74.2 us (0.981)
  Pallas kernels: 74.8 us -> 73.5 us
    pallas_call x1, Pallas kernels: 73.7 us -> 72.4 us  [on_device(): pl.pallas_call(kernel, out_shape=(jax.ShapeDtypeStruct((512, 512), BF16),...]
where the time goes in v7:
time: 74.2 us; the launch traced here: 74.1 us
  Pallas kernels  73.5 us (99%)
    pallas_call x1, Pallas kernels, on_device(): pl.pallas_call(kernel, out_shape=(jax.ShapeDtypeStruct((512, 512), BF16),...  72.4 us

profile of v7, /device:TPU:1, one launch (start us, length us, event | category | flops | bytes accessed | tf_op | source)
XLA Modules:
  0.0 74.1 jit_solution(11762531195343681106)
XLA Ops:
  0.6 72.4 %shard_map.95 = (bf16[512,512]{1,0:T(8,128)(2,1)S(1)}, f32[6,256,128]{2,1,0:T(8,128)S(1)}) custom-call(bf16[512,512]{1,0:T(8,128)(2,1)} %bitcast.13, bf16[2048,512]{1,0:T(8,128)(2,1)} %bitcast.9, bf16[3,256,512]{2,1,0:T(8,128)(2,1)} %bitcast.12, s32[1,6]{1,0:T(1,128)} %pat.1, s32[1,6]{1,0:T(1,128)} %off.1, f32[6,256,256]{2,1,0:T(8,128)} %bitcast.10, ...), custom_call_target="tpu_custom_call" | custom-call | tf_op jit(solution)/shard_map/pallas_call | solution.py:500
  73.0 1.1 %shard_map.96 = (bf16[512,512]{1,0:T(8,128)(2,1)}, f32[6,256,128]{2,1,0:T(8,128)}) custom-call(bf16[512,512]{1,0:T(8,128)(2,1)S(1)} %get-tuple-element.6.x, f32[6,256,128]{2,1,0:T(8,128)S(1)} %get-tuple-element.7.sol), custom_call_target="tpu_custom_call" | custom-call | tf_op jit(solution)/shard_map/pallas_call | solution.py:571
